TPU v7x, 32 devices: a whole 2x2x4 slice. The times are simulated.
32 devices in a mesh: lon: 4 (over z), lat: 8 (over y, x, core).
Axes of the slice: x: 2, y: 2, z: 4, core: 2. Of those that a mesh axis runs over, the one named last changes fastest.
Arguments:
- tracers: float32 [3, 8, 64, 512], P(None, None, 'lat', 'lon'), may hold values from -6 to 6
- cotangent: float32 [3, 8, 64, 512], P(None, None, 'lat', 'lon'), may hold values from -6 to 6
- east_vel: float32 [8, 64, 512], P(None, 'lat', 'lon'), may hold values from -0.3 to 0.3
- north_vel: float32 [8, 64, 512], P(None, 'lat', 'lon'), may hold values from -0.3 to 0.3
- sea_mask: int32 [64, 512], P('lat', 'lon'), may hold values 0 or 1
- level_count: int32 [64, 512], P('lat', 'lon'), may hold values from 1 to 8
Outputs:
- adj_tracers: float32 [3, 8, 64, 512], P(None, None, 'lat', 'lon')
- adj_east: float32 [8, 64, 512], P(None, 'lat', 'lon')
- adj_north: float32 [8, 64, 512], P(None, 'lat', 'lon')
All inputs are finite; a program needn't handle non-finite values. No bound on the sum of `sea_mask` on one device may be relied on, other than what follows from the above.
Results may differ from a plain program's by a relative error of at most 0.00002.
Values sent between devices are 32-bit elements; how exact they have to be, the bound alone decides.
No kernel may reach another device: no remote copies, remote signals or barrier semaphores. Data moves between devices by JAX's collectives and lax.ppermute only.
A program may use at most 64 MiB of HBM per device.

v0:
```python
import jax
import jax.numpy as jnp
from jax import lax
from jax.sharding import PartitionSpec as P

STEPS = 4


horiz_diff = 0.22
vert_diff = 0.05


def extended_2(cells, sides, width, closed):
    for axis, dim in sides:
        count = lax.axis_size(axis)
        ends = count if closed else count - 1
        head = lax.slice_in_dim(cells, 0, width, axis=dim)
        tail = lax.slice_in_dim(cells, cells.shape[dim] - width, cells.shape[dim], axis=dim)
        cells = jnp.concatenate(
            [
                lax.ppermute(tail, axis, [(i, (i + 1) % count) for i in range(ends)]),
                cells,
                lax.ppermute(head, axis, [((i + 1) % count, i) for i in range(ends)]),
            ],
            axis=dim,
        )
    return cells


def advance(tracer, east_field, north_field, wetness):
    row_part = tracer[..., 1:-1, :]
    row_wet = wetness[:, 1:-1, :]
    east_open = row_wet[:, :, :-1] * row_wet[:, :, 1:]
    east_flux = east_open * (
        east_field[:, 1:-1, :-1] * 0.5 * (row_part[..., :-1] + row_part[..., 1:])
        - horiz_diff * (row_part[..., 1:] - row_part[..., :-1])
    )
    column_part = tracer[..., :, 1:-1]
    column_wet = wetness[:, :, 1:-1]
    north_open = column_wet[:, :-1, :] * column_wet[:, 1:, :]
    north_flux = north_open * (
        north_field[:, :-1, 1:-1] * 0.5 * (column_part[..., :-1, :] + column_part[..., 1:, :])
        - horiz_diff * (column_part[..., 1:, :] - column_part[..., :-1, :])
    )
    centre = tracer[..., 1:-1, 1:-1]
    centre_wet = wetness[:, 1:-1, 1:-1]
    vertical_open = centre_wet[:-1] * centre_wet[1:]
    vertical_flux = vertical_open * vert_diff * (centre[..., 1:, :, :] - centre[..., :-1, :, :])
    nothing = jnp.zeros_like(centre[..., :1, :, :])
    mixing = jnp.concatenate([vertical_flux, nothing], -3) - jnp.concatenate(
        [nothing, vertical_flux], -3
    )
    return centre_wet * (
        centre
        - (east_flux[..., 1:] - east_flux[..., :-1])
        - (north_flux[..., 1:, :] - north_flux[..., :-1, :])
        + mixing
    )


def march_steps(initial, east_field, north_field, wetness):
    current = initial
    for repeat in range(STEPS):
        row_end = east_field.shape[1] - repeat
        col_end = east_field.shape[2] - repeat
        current = advance(
            current,
            east_field[:, repeat:row_end, repeat:col_end],
            north_field[:, repeat:row_end, repeat:col_end],
            wetness[:, repeat:row_end, repeat:col_end],
        )
    return current


def clear_outside(extended, rim_width):
    lat_place = lax.axis_index("lat")
    lat_total = lax.axis_size("lat")
    row_index = lax.broadcasted_iota(jnp.int32, extended.shape, 1)
    keep_cell = ((row_index >= rim_width) | (lat_place > 0)) & (
        (row_index < extended.shape[1] - rim_width) | (lat_place < lat_total - 1)
    )
    return jnp.where(keep_cell, extended, jnp.zeros_like(extended))


def extend_state(field_in, rim_width):
    extended = extended_2(field_in, (("lon", 2), ("lat", 1)), rim_width, True)
    return clear_outside(extended, rim_width)


def extend_static(field_in, rim_width):
    extended = extended_2(field_in, (("lon", 2), ("lat", 1)), rim_width, True)
    return clear_outside(extended, rim_width)


def return_rims(gradient, rim_width):
    lon_cols = gradient.shape[2] - 2 * rim_width
    lat_rows = gradient.shape[1] - 2 * rim_width
    margins = jnp.concatenate([gradient[..., :rim_width], gradient[..., lon_cols + rim_width :]], 2)
    arrived = extended_2(margins, (("lon", 2),), rim_width, True)
    inner_part = gradient[..., rim_width : lon_cols + rim_width]
    inner_part = inner_part.at[..., :rim_width].add(arrived[..., :rim_width])
    inner_part = inner_part.at[..., lon_cols - rim_width :].add(arrived[..., 3 * rim_width :])
    margins = jnp.concatenate([inner_part[:, :rim_width], inner_part[:, lat_rows + rim_width :]], 1)
    arrived = extended_2(margins, (("lat", 1),), rim_width, False)
    result = inner_part[:, rim_width : lat_rows + rim_width]
    result = result.at[:, :rim_width].add(arrived[:, :rim_width])
    return result.at[:, lat_rows - rim_width :].add(arrived[:, 3 * rim_width :])


def on_device(tracers, cotangent, east_vel, north_vel, sea_mask, level_count):
    tracer_count = tracers.shape[0]
    level_total = east_vel.shape[0]
    lat_rows = east_vel.shape[1]
    lon_cols = east_vel.shape[2]
    stacked_count = tracer_count * level_total
    level_index = lax.broadcasted_iota(jnp.int32, east_vel.shape, 0)
    wet_field = jnp.where(
        (sea_mask[None] == 1) & (level_index < level_count[None]), 1.0, 0.0
    ).astype(jnp.float32)
    static_fields = jnp.concatenate([east_vel, north_vel, wet_field], 0)
    state_flat = (stacked_count, lat_rows, lon_cols)
    static_wide = extend_static(static_fields, STEPS)
    east_wide = static_wide[:level_total]
    north_wide = static_wide[level_total : 2 * level_total]
    wet_wide = static_wide[2 * level_total :]
    widened = extend_state(tracers.reshape(state_flat), STEPS).reshape(
        tracer_count, level_total, lat_rows + 2 * STEPS, lon_cols + 2 * STEPS
    )

    def deep_march(initial, east_field, north_field):
        return march_steps(initial, east_field, north_field, wet_wide)

    ignored, pullback = jax.vjp(deep_march, widened, east_wide, north_wide)
    back_state, back_east, back_north = pullback(cotangent)
    combined = jnp.concatenate(
        [back_state.reshape((stacked_count,) + back_state.shape[2:]), back_east, back_north], 0
    )
    returned = return_rims(combined, STEPS)
    adjoint = returned[:stacked_count].reshape(tracers.shape)
    return (
        adjoint,
        returned[stacked_count : stacked_count + level_total],
        returned[stacked_count + level_total :],
    )


def solution(mesh):
    placed = (
        P(None, None, "lat", "lon"),
        P(None, None, "lat", "lon"),
        P(None, "lat", "lon"),
        P(None, "lat", "lon"),
        P("lat", "lon"),
        P("lat", "lon"),
    )
    return jax.shard_map(
        on_device,
        mesh=mesh,
        in_specs=placed,
        out_specs=(P(None, None, "lat", "lon"), P(None, "lat", "lon"), P(None, "lat", "lon")),
        check_vma=False,
    )
```

profile of v0, /device:TPU:3, one launch (start us, length us, event | category | flops | bytes accessed | tf_op | source)
XLA Modules:
  0.0 70.1 jit_solution(5267702251486694149)
XLA Ops:
  0.7 0.7 %broadcast_compare_fusion = pred[8,128]{1,0:T(8,128)(4,1)S(1)} fusion(s32[8,128]{1,0:T(8,128)} %param.18), kind=kLoop, calls=%fused_computation.150 | loop fusion | flops 1024 | bytes 5120 | tf_op jit(solution)/shard_map/eq | solution.py:118
  1.4 0.8 %pad_maximum_fusion.3 = f32[24,8,128]{2,1,0:T(8,128)S(1)} fusion(f32[8,8,128]{2,1,0:T(8,128)S(1)} %fusion.33, f32[8,8,128]{2,1,0:T(8,128)S(1)} %copy-done.1, f32[8,8,128]{2,1,0:T(8,128)} %param.16), kind=kLoop, calls=%fused_computation.124 | loop fusion | flops 49152 | bytes 196608 | tf_op jit(solution)/shard_map/concatenate | solution.py:120
  2.3 1.3 %collective-permute-start = (f32[24,8,4]{2,1,0:T(8,128)S(1)}, f32[24,8,4]{2,1,0:T(8,128)S(1)}, u32[]{:S(2)}, u32[]{:S(2)}) collective-permute-start(f32[24,8,4]{2,1,0:T(8,128)S(1)} %get-tuple-element.132), channel_id=1, source_target_pairs={{0,8},{8,16},{16,24},{24,0},{1,9},{9,17},{17,25},{25,1},{2,10},{10... | collective-permute-start | bytes 9224 | tf_op jit(solution)/shard_map/ppermute | solution.py:21
  3.6 2.1 %collective-permute-start.1 = (f32[24,8,4]{2,1,0:T(8,128)S(1)}, f32[24,8,4]{2,1,0:T(8,128)S(1)}, u32[]{:S(2)}, u32[]{:S(2)}) collective-permute-start(f32[24,8,4]{2,1,0:T(8,128)S(1)} %get-tuple-element.133), channel_id=1, source_target_pairs={{8,0},{16,8},{24,16},{0,24},{9,1},{17,9},{25,17},{1,25},{10,2},{18... | collective-permute-start | bytes 9224 | tf_op jit(solution)/shard_map/ppermute | solution.py:23
  5.9 3.3 %collective-permute-start.5 = (f32[24,8,4]{2,1,0:T(8,128)S(1)}, f32[24,8,4]{2,1,0:T(8,128)S(1)}, u32[]{:S(2)}, u32[]{:S(2)}) collective-permute-start(f32[24,8,4]{2,1,0:T(8,128)S(1)} %get-tuple-element.135), channel_id=1, source_target_pairs={{8,0},{16,8},{24,16},{0,24},{9,1},{17,9},{25,17},{1,25},{10,2},{18... | collective-permute-start | bytes 9224 | tf_op jit(solution)/shard_map/ppermute | solution.py:23
  9.1 0.7 %collective-permute-done.1 = f32[24,8,4]{2,1,0:T(8,128)S(1)} collective-permute-done((f32[24,8,4]{2,1,0:T(8,128)S(1)}, f32[24,8,4]{2,1,0:T(8,128)S(1)}, u32[]{:S(2)}, u32[]{:S(2)}) %collective-permute-start.1) | collective-permute-done | bytes 3104 | tf_op jit(solution)/shard_map/ppermute | solution.py:23
  10.1 3.6 %collective-permute-start.2 = (f32[24,4,136]{2,1,0:T(4,128)S(1)}, f32[24,4,136]{2,1,0:T(4,128)S(1)}, u32[]{:S(2)}, u32[]{:S(2)}) collective-permute-start(f32[24,4,136]{2,1,0:T(4,128)S(1)} %get-tuple-element.125), channel_id=1, source_target_pairs={{0,1},{1,2},{2,3},{3,4},{4,5},{5,6},{6,7},{7,0},{8,9},{9,10},{10,1... | collective-permute-start | bytes 156680 | tf_op jit(solution)/shard_map/ppermute | solution.py:21
  13.7 0.4 collective-permute-done.5
  14.3 2.3 %collective-permute-start.6 = (f32[24,4,136]{2,1,0:T(4,128)S(1)}, f32[24,4,136]{2,1,0:T(4,128)S(1)}, u32[]{:S(2)}, u32[]{:S(2)}) collective-permute-start(f32[24,4,136]{2,1,0:T(4,128)S(1)} %get-tuple-element.127), channel_id=1, source_target_pairs={{0,1},{1,2},{2,3},{3,4},{4,5},{5,6},{6,7},{7,0},{8,9},{9,10},{10,1... | collective-permute-start | bytes 156680 | tf_op jit(solution)/shard_map/ppermute | solution.py:21
  16.6 2.0 %collective-permute-done.3 = f32[24,4,136]{2,1,0:T(4,128)S(1)} collective-permute-done((f32[24,4,136]{2,1,0:T(4,128)S(1)}, f32[24,4,136]{2,1,0:T(4,128)S(1)}, u32[]{:S(2)}, u32[]{:S(2)}) %collective-permute-start.3) | collective-permute-done | bytes 52256 | tf_op jit(solution)/shard_map/ppermute | solution.py:23
  20.7 0.7 %copy-done.3 = f32[3,8,8,128]{3,2,1,0:T(8,128)S(1)} copy-done((f32[3,8,8,128]{3,2,1,0:T(8,128)S(1)}, f32[3,8,8,128]{3,2,1,0:T(8,128)}, u32[]{:S(2)}) %copy-start.3) | copy-done | bytes 98328
  22.7 0.3 fusion.10
  24.2 0.3 fusion.6
  25.0 0.4 multiply_reduce_fusion.5
  25.4 0.3 multiply_reduce_fusion.2
  25.7 0.4 fusion.2
  26.9 0.3 pad_add_fusion.7
  27.5 0.3 multiply_reduce_fusion.4
  28.0 0.3 negate_multiply_fusion.3
  29.0 0.3 fusion.43
  30.0 0.3 negate_multiply_fusion.1
  31.8 1.5 %collective-permute-start.8 = (f32[40,16,4]{2,1,0:T(8,128)S(1)}, f32[40,16,4]{2,1,0:T(8,128)S(1)}, u32[]{:S(2)}, u32[]{:S(2)}) collective-permute-start(f32[40,16,4]{2,1,0:T(8,128)S(1)} %get-tuple-element.84), channel_id=1, source_target_pairs={{0,8},{8,16},{16,24},{24,0},{1,9},{9,17},{17,25},{25,1},{2,10},{10... | collective-permute-start | bytes 30728 | tf_op jit(solution)/shard_map/ppermute | solution.py:21
  33.4 2.1 %collective-permute-start.9 = (f32[40,16,4]{2,1,0:T(8,128)S(1)}, f32[40,16,4]{2,1,0:T(8,128)S(1)}, u32[]{:S(2)}, u32[]{:S(2)}) collective-permute-start(f32[40,16,4]{2,1,0:T(8,128)S(1)} %get-tuple-element.83), channel_id=1, source_target_pairs={{8,0},{16,8},{24,16},{0,24},{9,1},{17,9},{25,17},{1,25},{10,2},{18... | collective-permute-start | bytes 30728 | tf_op jit(solution)/shard_map/ppermute | solution.py:23
  35.5 7.6 %collective-permute-done.8 = f32[40,16,4]{2,1,0:T(8,128)S(1)} collective-permute-done((f32[40,16,4]{2,1,0:T(8,128)S(1)}, f32[40,16,4]{2,1,0:T(8,128)S(1)}, u32[]{:S(2)}, u32[]{:S(2)}) %collective-permute-start.8) | collective-permute-done | bytes 10272 | tf_op jit(solution)/shard_map/ppermute | solution.py:21
  43.2 4.3 %scatter-add.14 = f32[40,16,128]{2,1,0:T(8,128)S(1)} dynamic-update-slice(f32[40,16,128]{2,1,0:T(8,128)S(1)} %slice.657, f32[40,16,4]{2,1,0:T(8,128)S(1)} %slice_add_fusion.10, s32[]{:T(128)} %constant.141.clone.1, s32[]{:T(128)} %constant.141.clone.1, s32[]{:T(128)} %constant.141.clone.1) | dynamic-update-slice | bytes 20484 | tf_op jit(solution)/shard_map/scatter-add | solution.py:101
  47.6 1.2 %collective-permute-done.9 = f32[40,16,4]{2,1,0:T(8,128)S(1)} collective-permute-done((f32[40,16,4]{2,1,0:T(8,128)S(1)}, f32[40,16,4]{2,1,0:T(8,128)S(1)}, u32[]{:S(2)}, u32[]{:S(2)}) %collective-permute-start.9) | collective-permute-done | bytes 10272 | tf_op jit(solution)/shard_map/ppermute | solution.py:23
  48.9 9.3 %scatter-add.15 = f32[40,16,128]{2,1,0:T(8,128)S(1)} dynamic-update-slice(f32[40,16,128]{2,1,0:T(8,128)S(1)} %scatter-add.14, f32[40,16,4]{2,1,0:T(8,128)S(1)} %slice_add_fusion.9, s32[]{:T(128)} %constant.141.clone.1, s32[]{:T(128)} %constant.141.clone.1, s32[]{:T(128)} %constant.150.clone.1) | dynamic-update-slice | bytes 20484 | tf_op jit(solution)/shard_map/scatter-add | solution.py:102
  58.3 3.8 %collective-permute-start.10 = (f32[40,4,128]{2,1,0:T(4,128)S(1)}, f32[40,4,128]{2,1,0:T(4,128)S(1)}, u32[]{:S(2)}, u32[]{:S(2)}) collective-permute-start(f32[40,4,128]{2,1,0:T(4,128)S(1)} %get-tuple-element.122), channel_id=1, source_target_pairs={{0,1},{1,2},{2,3},{3,4},{4,5},{5,6},{6,7},{8,9},{9,10},{10,11},{11... | collective-permute-start | bytes 245768 | tf_op jit(solution)/shard_map/ppermute | solution.py:21
  62.2 1.9 %collective-permute-start.11 = (f32[40,4,128]{2,1,0:T(4,128)S(1)}, f32[40,4,128]{2,1,0:T(4,128)S(1)}, u32[]{:S(2)}, u32[]{:S(2)}) collective-permute-start(f32[40,4,128]{2,1,0:T(4,128)S(1)} %get-tuple-element.121), channel_id=1, source_target_pairs={{1,0},{2,1},{3,2},{4,3},{5,4},{6,5},{7,6},{9,8},{10,9},{11,10},{12... | collective-permute-start | bytes 245768 | tf_op jit(solution)/shard_map/ppermute | solution.py:23
  64.1 4.7 %collective-permute-done.11 = f32[40,4,128]{2,1,0:T(4,128)S(1)} collective-permute-done((f32[40,4,128]{2,1,0:T(4,128)S(1)}, f32[40,4,128]{2,1,0:T(4,128)S(1)}, u32[]{:S(2)}, u32[]{:S(2)}) %collective-permute-start.11) | collective-permute-done | bytes 81952 | tf_op jit(solution)/shard_map/ppermute | solution.py:23
  68.9 0.6 fusion.59
  69.5 0.6 slice.667
  (98 shorter events, 10.1 us)
Async XLA Ops:
  0.6 0.7 %copy-start.4 = (s32[8,128]{1,0:T(8,128)S(1)}, s32[8,128]{1,0:T(8,128)}, u32[]{:S(2)}) copy-start(s32[8,128]{1,0:T(8,128)} %param.19) | copy-start | bytes 12292
  0.6 0.8 %copy-start.1 = (f32[8,8,128]{2,1,0:T(8,128)S(1)}, f32[8,8,128]{2,1,0:T(8,128)}, u32[]{:S(2)}) copy-start(f32[8,8,128]{2,1,0:T(8,128)} %param.17) | copy-start | bytes 98308
  2.2 3.5 %copy-start = (f32[3,8,8,128]{3,2,1,0:T(8,128)S(1)}, f32[3,8,8,128]{3,2,1,0:T(8,128)}, u32[]{:S(2)}) copy-start(f32[3,8,8,128]{3,2,1,0:T(8,128)} %param.14) | copy-start | bytes 294916
  2.3 6.9 %collective-permute-start = (f32[24,8,4]{2,1,0:T(8,128)S(1)}, f32[24,8,4]{2,1,0:T(8,128)S(1)}, u32[]{:S(2)}, u32[]{:S(2)}) collective-permute-start(f32[24,8,4]{2,1,0:T(8,128)S(1)} %get-tuple-element.132), channel_id=1, source_target_pairs={{0,8},{8,16},{16,24},{24,0},{1,9},{9,17},{17,25},{25,1},{2,10},{10... | collective-permute-start | bytes 9224 | tf_op jit(solution)/shard_map/ppermute | solution.py:21
  3.6 6.3 %collective-permute-start.1 = (f32[24,8,4]{2,1,0:T(8,128)S(1)}, f32[24,8,4]{2,1,0:T(8,128)S(1)}, u32[]{:S(2)}, u32[]{:S(2)}) collective-permute-start(f32[24,8,4]{2,1,0:T(8,128)S(1)} %get-tuple-element.133), channel_id=1, source_target_pairs={{8,0},{16,8},{24,16},{0,24},{9,1},{17,9},{25,17},{1,25},{10,2},{18... | collective-permute-start | bytes 9224 | tf_op jit(solution)/shard_map/ppermute | solution.py:23
  5.7 4.2 %copy-start.2 = (f32[8,8,128]{2,1,0:T(8,128)S(1)}, f32[8,8,128]{2,1,0:T(8,128)}, u32[]{:S(2)}) copy-start(f32[8,8,128]{2,1,0:T(8,128)} %param.16) | copy-start | bytes 98308
  5.8 7.9 %collective-permute-start.4 = (f32[24,8,4]{2,1,0:T(8,128)S(1)}, f32[24,8,4]{2,1,0:T(8,128)S(1)}, u32[]{:S(2)}, u32[]{:S(2)}) collective-permute-start(f32[24,8,4]{2,1,0:T(8,128)S(1)} %get-tuple-element.134), channel_id=1, source_target_pairs={{0,8},{8,16},{16,24},{24,0},{1,9},{9,17},{17,25},{25,1},{2,10},{10... | collective-permute-start | bytes 9224 | tf_op jit(solution)/shard_map/ppermute | solution.py:21
  5.9 8.2 %collective-permute-start.5 = (f32[24,8,4]{2,1,0:T(8,128)S(1)}, f32[24,8,4]{2,1,0:T(8,128)S(1)}, u32[]{:S(2)}, u32[]{:S(2)}) collective-permute-start(f32[24,8,4]{2,1,0:T(8,128)S(1)} %get-tuple-element.135), channel_id=1, source_target_pairs={{8,0},{16,8},{24,16},{0,24},{9,1},{17,9},{25,17},{1,25},{10,2},{18... | collective-permute-start | bytes 9224 | tf_op jit(solution)/shard_map/ppermute | solution.py:23
  10.1 6.5 %collective-permute-start.2 = (f32[24,4,136]{2,1,0:T(4,128)S(1)}, f32[24,4,136]{2,1,0:T(4,128)S(1)}, u32[]{:S(2)}, u32[]{:S(2)}) collective-permute-start(f32[24,4,136]{2,1,0:T(4,128)S(1)} %get-tuple-element.125), channel_id=1, source_target_pairs={{0,1},{1,2},{2,3},{3,4},{4,5},{5,6},{6,7},{7,0},{8,9},{9,10},{10,1... | collective-permute-start | bytes 156680 | tf_op jit(solution)/shard_map/ppermute | solution.py:21
  13.7 4.9 %collective-permute-start.3 = (f32[24,4,136]{2,1,0:T(4,128)S(1)}, f32[24,4,136]{2,1,0:T(4,128)S(1)}, u32[]{:S(2)}, u32[]{:S(2)}) collective-permute-start(f32[24,4,136]{2,1,0:T(4,128)S(1)} %get-tuple-element.126), channel_id=1, source_target_pairs={{1,0},{2,1},{3,2},{4,3},{5,4},{6,5},{7,6},{0,7},{9,8},{10,9},{11,1... | collective-permute-start | bytes 156680 | tf_op jit(solution)/shard_map/ppermute | solution.py:23
  14.3 7.5 %collective-permute-start.6 = (f32[24,4,136]{2,1,0:T(4,128)S(1)}, f32[24,4,136]{2,1,0:T(4,128)S(1)}, u32[]{:S(2)}, u32[]{:S(2)}) collective-permute-start(f32[24,4,136]{2,1,0:T(4,128)S(1)} %get-tuple-element.127), channel_id=1, source_target_pairs={{0,1},{1,2},{2,3},{3,4},{4,5},{5,6},{6,7},{7,0},{8,9},{9,10},{10,1... | collective-permute-start | bytes 156680 | tf_op jit(solution)/shard_map/ppermute | solution.py:21
  16.6 5.2 %collective-permute-start.7 = (f32[24,4,136]{2,1,0:T(4,128)S(1)}, f32[24,4,136]{2,1,0:T(4,128)S(1)}, u32[]{:S(2)}, u32[]{:S(2)}) collective-permute-start(f32[24,4,136]{2,1,0:T(4,128)S(1)} %get-tuple-element.128), channel_id=1, source_target_pairs={{1,0},{2,1},{3,2},{4,3},{5,4},{6,5},{7,6},{0,7},{9,8},{10,9},{11,1... | collective-permute-start | bytes 156680 | tf_op jit(solution)/shard_map/ppermute | solution.py:23
  20.5 0.9 %copy-start.3 = (f32[3,8,8,128]{3,2,1,0:T(8,128)S(1)}, f32[3,8,8,128]{3,2,1,0:T(8,128)}, u32[]{:S(2)}) copy-start(f32[3,8,8,128]{3,2,1,0:T(8,128)} %param.15) | copy-start | bytes 294916
  31.8 11.3 %collective-permute-start.8 = (f32[40,16,4]{2,1,0:T(8,128)S(1)}, f32[40,16,4]{2,1,0:T(8,128)S(1)}, u32[]{:S(2)}, u32[]{:S(2)}) collective-permute-start(f32[40,16,4]{2,1,0:T(8,128)S(1)} %get-tuple-element.84), channel_id=1, source_target_pairs={{0,8},{8,16},{16,24},{24,0},{1,9},{9,17},{17,25},{25,1},{2,10},{10... | collective-permute-start | bytes 30728 | tf_op jit(solution)/shard_map/ppermute | solution.py:21
  33.4 15.4 %collective-permute-start.9 = (f32[40,16,4]{2,1,0:T(8,128)S(1)}, f32[40,16,4]{2,1,0:T(8,128)S(1)}, u32[]{:S(2)}, u32[]{:S(2)}) collective-permute-start(f32[40,16,4]{2,1,0:T(8,128)S(1)} %get-tuple-element.83), channel_id=1, source_target_pairs={{8,0},{16,8},{24,16},{0,24},{9,1},{17,9},{25,17},{1,25},{10,2},{18... | collective-permute-start | bytes 30728 | tf_op jit(solution)/shard_map/ppermute | solution.py:23
  58.3 5.8 %collective-permute-start.10 = (f32[40,4,128]{2,1,0:T(4,128)S(1)}, f32[40,4,128]{2,1,0:T(4,128)S(1)}, u32[]{:S(2)}, u32[]{:S(2)}) collective-permute-start(f32[40,4,128]{2,1,0:T(4,128)S(1)} %get-tuple-element.122), channel_id=1, source_target_pairs={{0,1},{1,2},{2,3},{3,4},{4,5},{5,6},{6,7},{8,9},{9,10},{10,11},{11... | collective-permute-start | bytes 245768 | tf_op jit(solution)/shard_map/ppermute | solution.py:21
  62.2 6.7 %collective-permute-start.11 = (f32[40,4,128]{2,1,0:T(4,128)S(1)}, f32[40,4,128]{2,1,0:T(4,128)S(1)}, u32[]{:S(2)}, u32[]{:S(2)}) collective-permute-start(f32[40,4,128]{2,1,0:T(4,128)S(1)} %get-tuple-element.121), channel_id=1, source_target_pairs={{1,0},{2,1},{3,2},{4,3},{5,4},{6,5},{7,6},{9,8},{10,9},{11,10},{12... | collective-permute-start | bytes 245768 | tf_op jit(solution)/shard_map/ppermute | solution.py:23
where the time goes:
time: 70.5 us; the launch traced here: 70.1 us
  starting transfers between devices  22 us (31%)
  waiting for transfers between devices  16.7 us (24%)
  local copies, waits for them, and re-layouts  16.6 us (24%)
  other arithmetic  13.6 us (19%)
  between operations  1.3 us (2%)
    ppermute x6, starting transfers between devices, extended_2(): lax.ppermute(tail, axis, [(i, (i + 1) % count) for i in range(ends)])  12.7 us
    ppermute x6, starting transfers between devices, extended_2(): lax.ppermute(head, axis, [((i + 1) % count, i) for i in range(ends)])  9.34 us
    scatter-add x1, local copies, waits for them, and re-layouts, return_rims(): inner_part.at[..., lon_cols - rim_width:].add(arrived[..., 3 * rim_width:])  9.31 us
    ppermute x6, waiting for transfers between devices, extended_2(): lax.ppermute(head, axis, [((i + 1) % count, i) for i in range(ends)])  9.06 us
    ppermute x6, waiting for transfers between devices, extended_2(): lax.ppermute(tail, axis, [(i, (i + 1) % count) for i in range(ends)])  7.6 us
    scatter-add x1, local copies, waits for them, and re-layouts, return_rims(): inner_part = inner_part.at[..., :rim_width].add(arrived[..., :rim_width])  4.33 us
  transfers between devices with their start and end apart: 12, of which 6 were waited for; matrix products, arithmetic and copies ran while one was open for 11% of the time, Pallas kernels for 0%

commit v1 on v0

v1 whole, which is shorter than its diff:
```python
import jax
import jax.numpy as jnp
from jax import lax
from jax.experimental import pallas as pl
from jax.experimental.pallas import tpu as pltpu
from jax.sharding import PartitionSpec as P

STEPS = 4
HORIZ = 0.22
VERT = 0.05

ROWS = 8
LANES = 128
RIM = 4
SLOT = 16
F32 = jnp.float32
VMEM = 8 << 20


def iota(axis):
    return lax.broadcasted_iota(jnp.int32, (ROWS, LANES), axis)


def lane_roll(x, shift):
    shift %= LANES
    return x if shift == 0 else pltpu.roll(x, shift, 1)


def row_roll(x, shift):
    return pltpu.roll(x, shift % ROWS, 0)


def east(x):
    return lane_roll(x, -1)


def west(x):
    return lane_roll(x, 1)


def north(own, rim, last):
    a, b = row_roll(own, -1), row_roll(rim, -1)
    return jnp.where(last, b, a), jnp.where(last, a, b)


def south(own, rim, first):
    a, b = row_roll(own, 1), row_roll(rim, 1)
    return jnp.where(first, b, a), jnp.where(first, a, b)


def odd_row():
    return lax.rem(lax.axis_index("lat"), 2)


def wet_count(mask, count):
    return jnp.where(mask == 1, count, 0).astype(F32)


def edge_of(planes):
    slot = iota(1) // SLOT
    out = None
    for k, plane in enumerate(planes):
        moved = lane_roll(plane, SLOT * k + SLOT // 2)
        out = moved if out is None else jnp.where(slot == k, moved, out)
    return out


def inside_rows(rim):
    place, total = lax.axis_index("lat"), lax.axis_size("lat")
    sub = iota(0)
    keep = ((sub >= RIM) | (place < total - 1)) & ((sub < RIM) | (place > 0))
    return jnp.where(keep, rim, 0.0)


def pack_kernel(*refs):
    args, here, (pair_a, pair_b, to_west, to_east, edge, sems) = refs[:6], refs[6:12], refs[12:]
    copies = [pltpu.make_async_copy(a, b, sems.at[i]) for i, (a, b) in enumerate(zip(args, here))]
    for copy in copies:
        copy.start()
    for copy in copies:
        copy.wait()
    trac, cot, east_vel, north_vel, mask, count = here
    n_trac, lev = trac.shape[:2]
    upper = (iota(0) // RIM) != odd_row()

    def pair(index, p, q):
        q = row_roll(q, RIM)
        pair_a[index] = jnp.where(upper, p, q)
        pair_b[index] = jnp.where(upper, q, p)

    for t in range(n_trac):
        for k in range(lev):
            pair(t * lev + k, trac[t, k], cot[t, k])
    for k in range(lev):
        pair(n_trac * lev + k, east_vel[k], north_vel[k])
    wet = wet_count(mask[...], count[...])
    pair_a[(n_trac + 1) * lev] = wet
    pair_b[(n_trac + 1) * lev] = wet

    fields = [[trac[t, k] for k in range(lev)] for t in range(n_trac)]
    fields += [[cot[t, k] for k in range(lev)] for t in range(n_trac)]
    fields += [[ref[k] for k in range(lev)] for ref in (east_vel, north_vel)]
    fields += [[wet] * lev]
    quarter = (iota(1) % SLOT) // RIM
    west_out, east_out = {}, {}
    for f, planes in enumerate(fields):
        e = edge_of(planes)
        edge[f] = e
        d, g = divmod(f, SLOT // RIM)
        if f == len(fields) - 1 and g == 0:
            west_out[d] = east_out[d] = e
            continue
        moved = lane_roll(e, RIM * g - 8)
        if g == 0:
            west_out[d] = east_out[d] = moved
        else:
            west_out[d] = jnp.where(quarter == g, moved, west_out[d])
            east_out[d] = jnp.where(quarter == g - 1, moved, east_out[d])
    for d in west_out:
        to_west[d] = west_out[d]
        to_east[d] = east_out[d]


def corner_kernel(from_west, from_east, pair_a, pair_b):
    upper = (iota(0) // RIM) != odd_row()
    for d in range(from_west.shape[0]):
        p, q = from_west[d], row_roll(from_east[d], RIM)
        pair_a[d] = jnp.where(upper, p, q)
        pair_b[d] = jnp.where(upper, q, p)


def unpair(a, b):
    from_a = (iota(0) // RIM) == odd_row()
    return jnp.where(from_a, a, b), row_roll(jnp.where(from_a, b, a), RIM)


def coefficients(wet, wet_up, wet_down, u, v):
    sub = iota(0)
    first, last = sub == 0, sub == ROWS - 1
    north_wet = north(*wet, last)
    out = []
    for h in range(2):
        east_open = wet[h] * east(wet[h])
        north_open = wet[h] * north_wet[h]
        hu, hv = 0.5 * u[h], 0.5 * v[h]
        c = dict(
            east_open=east_open,
            north_open=north_open,
            p=east_open * (hu + HORIZ),
            q=east_open * (HORIZ - hu),
            r=north_open * (hv + HORIZ),
            s=north_open * (HORIZ - hv),
            up=None if wet_up is None else (VERT * wet[h]) * wet_up[h],
            down=None if wet_down is None else (VERT * wet[h]) * wet_down[h],
        )
        c["pw"], c["qw"] = west(c["p"]), west(c["q"])
        out.append(c)
    rs, ss = south(out[0]["r"], out[1]["r"], first), south(out[0]["s"], out[1]["s"], first)
    for h in range(2):
        c = out[h]
        c["rs"], c["ss"] = rs[h], ss[h]
        centre = wet[h] - ((c["p"] + c["qw"]) + (c["r"] + c["ss"]))
        for side in ("up", "down"):
            if c[side] is not None:
                centre = centre - c[side]
        c["centre"] = centre
    return out


FORWARD = ("q", "pw", "s", "rs")
BACKWARD = ("p", "qw", "r", "ss")


def combine(coef, names, x, e, w, n, s, up, down):
    out = (coef("centre") * x + coef(names[0]) * e) + (coef(names[1]) * w + coef(names[2]) * n)
    out = out + coef(names[3]) * s
    if up is not None:
        out = out + coef("up") * up
    if down is not None:
        out = out + coef("down") * down
    return out


COEFS = ("centre", "p", "q", "pw", "qw", "r", "s", "rs", "ss", "up", "down", "east_open", "north_open")


def main_kernel(trac, cot, east_vel, north_vel, mask, count, pair_a, pair_b, adj_t, adj_e, adj_n, edge_rim, state, sums, coef):
    n_trac, lev = trac.shape[:2]
    sub = iota(0)
    first, last = sub == 0, sub == ROWS - 1

    rims = {}
    for t in range(n_trac):
        for k in range(lev):
            c, b = unpair(pair_a[t * lev + k], pair_b[t * lev + k])
            state[0, t, k, 0] = trac[t, k]
            state[0, t, k, 1] = c
            state[2, t, k, 0] = cot[t, k]
            state[2, t, k, 1] = b
            rims[t, k], rims[n_trac + t, k] = c, b
    wet_at = (n_trac + 1) * lev
    count_own = wet_count(mask[...], count[...])
    count_rim = inside_rows(unpair(pair_a[wet_at], pair_b[wet_at])[0])
    wet = [tuple(jnp.where(x > k, 1.0, 0.0) for x in (count_own, count_rim)) for k in range(lev)]
    for k in range(lev):
        u_rim, v_rim = unpair(pair_a[n_trac * lev + k], pair_b[n_trac * lev + k])
        rims[2 * n_trac, k], rims[2 * n_trac + 1, k] = u_rim, v_rim
        rims[2 * n_trac + 2, k] = count_rim
        made = coefficients(
            wet[k],
            wet[k + 1] if k + 1 < lev else None,
            wet[k - 1] if k else None,
            (east_vel[k], u_rim),
            (north_vel[k], v_rim),
        )
        for h in range(2):
            for i, name in enumerate(COEFS):
                if made[h][name] is not None:
                    coef[i, k, h] = made[h][name]
    for f in range(2 * n_trac + 3):
        edge_rim[f] = edge_of([rims[f, k] for k in range(lev)])

    def neighbours(buf, t, k):
        own, rim = state[buf, t, k, 0], state[buf, t, k, 1]
        n, s = north(own, rim, last), south(own, rim, first)
        return (own, rim), (east(own), east(rim)), (west(own), west(rim)), n, s

    def apply(buf, t, k, near, names, halves):
        x, e, w, n, s = near
        for h in halves:
            up = state[buf, t, k + 1, h] if k + 1 < lev else None
            down = state[buf, t, k - 1, h] if k else None
            get = lambda name: coef[COEFS.index(name), k, h]
            yield h, combine(get, names, x[h], e[h], w[h], n[h], s[h], up, down)

    for step in range(STEPS):
        src, dst = step % 2, (step + 1) % 2
        for k in range(lev):
            for t in range(n_trac):
                if step < STEPS - 1:
                    near = neighbours(src, t, k)
                    for h, new in apply(src, t, k, near, FORWARD, (0, 1)):
                        state[dst, t, k, h] = new
                    x, e, n = near[0][0], near[1][0], near[3][0]
                else:
                    x, rim = state[src, t, k, 0], state[src, t, k, 1]
                    e, n = east(x), north(x, rim, last)[0]
                sums[step, 0, t, k] = x + e
                sums[step, 1, t, k] = x + n
    for step in reversed(range(STEPS)):
        src, dst = 2 + (STEPS - 1 - step) % 2, 2 + (STEPS - step) % 2
        for k in range(lev):
            acc_e = acc_n = None
            for t in range(n_trac):
                near = neighbours(src, t, k)
                for h, new in apply(src, t, k, near, BACKWARD, (0, 1) if step else (0,)):
                    if step:
                        state[dst, t, k, h] = new
                    else:
                        adj_t[t, k] = new
                x, e, n = near[0][0], near[1][0], near[3][0]
                term_e = sums[step, 0, t, k] * (e - x)
                term_n = sums[step, 1, t, k] * (n - x)
                acc_e = term_e if acc_e is None else acc_e + term_e
                acc_n = term_n if acc_n is None else acc_n + term_n
            if step < STEPS - 1:
                acc_e, acc_n = acc_e + adj_e[k], acc_n + adj_n[k]
            if step == 0:
                acc_e = acc_e * (0.5 * coef[COEFS.index("east_open"), k, 0])
                acc_n = acc_n * (0.5 * coef[COEFS.index("north_open"), k, 0])
            adj_e[k] = acc_e
            adj_n[k] = acc_n


def edge_kernel(edge, edge_rim, from_west, from_east, pair_a, pair_b, main_t, main_e, main_n, adj_t, adj_e, adj_n):
    n_trac, lev = main_t.shape[:2]
    n_fields = edge.shape[0]
    sub, lane = iota(0), iota(1)
    first, last = sub == 0, sub == ROWS - 1
    quarter = (lane % SLOT) // RIM
    corners = [unpair(pair_a[d], pair_b[d]) for d in range(from_west.shape[0])]

    def field(f, side):
        d, g = divmod(f, SLOT // RIM)
        shift = 0 if f == n_fields - 1 and g == 0 else 8 - RIM * g
        sent = (from_west, from_east)[side]
        own = jnp.where(quarter == 1 + side, lane_roll(sent[d], shift), edge[f])
        rim = jnp.where(quarter == 1 + side, lane_roll(corners[d][side], shift), edge_rim[f])
        return own, rim

    level = lane // SLOT
    out_e, out_n, out_t = [], [], []
    for side in range(2):
        own, rim = field(n_fields - 1, side)
        levels = level.astype(F32)
        wet = tuple(jnp.where(x > levels, 1.0, 0.0) for x in (own, inside_rows(rim)))
        up = tuple(jnp.where(level < lev - 1, lane_roll(x, -SLOT), 0.0) for x in wet)
        down = tuple(jnp.where(level > 0, lane_roll(x, SLOT), 0.0) for x in wet)
        made = coefficients(wet, up, down, field(2 * n_trac, side), field(2 * n_trac + 1, side))

        def near(x):
            n, s = north(*x, last), south(*x, first)
            return x, tuple(map(east, x)), tuple(map(west, x)), n, s

        def apply(about, names, halves):
            x, e, w, n, s = about
            out = []
            for h in halves:
                up, down = lane_roll(x[h], -SLOT), lane_roll(x[h], SLOT)
                out.append(combine(made[h].__getitem__, names, x[h], e[h], w[h], n[h], s[h], up, down))
            return tuple(out)

        state = [field(t, side) for t in range(n_trac)]
        lam = [field(n_trac + t, side) for t in range(n_trac)]
        sums = []
        for step in range(STEPS):
            about = [near(x) for x in state]
            sums.append([(a[0][0] + a[1][0], a[0][0] + a[3][0]) for a in about])
            if step < STEPS - 1:
                state = [apply(a, FORWARD, (0, 1)) for a in about]
        acc_e = acc_n = None
        for step in reversed(range(STEPS)):
            about = [near(x) for x in lam]
            for t, a in enumerate(about):
                x, e, n = a[0][0], a[1][0], a[3][0]
                term_e, term_n = sums[step][t][0] * (e - x), sums[step][t][1] * (n - x)
                acc_e = term_e if acc_e is None else acc_e + term_e
                acc_n = term_n if acc_n is None else acc_n + term_n
            lam = [apply(a, BACKWARD, (0, 1) if step else (0,)) for a in about]
        out_t.append([x[0] for x in lam])
        out_e.append(acc_e * (0.5 * made[0]["east_open"]))
        out_n.append(acc_n * (0.5 * made[0]["north_open"]))

    at_west = quarter >= 2
    margin = (lane < RIM) | (lane >= LANES - RIM)

    def put(ref, index, k, both, main):
        ref[index] = jnp.where(margin, lane_roll(both, -(SLOT * k + SLOT // 2)), main[index])

    for t in range(n_trac):
        both = jnp.where(at_west, out_t[0][t], out_t[1][t])
        for k in range(lev):
            put(adj_t, (t, k), k, both, main_t)
    for ref, out, main in ((adj_e, out_e, main_e), (adj_n, out_n, main_n)):
        both = jnp.where(at_west, *out)
        for k in range(lev):
            put(ref, (k,), k, both, main)


def call(body, outs, args, scratch=(), space=pltpu.VMEM):
    shapes = [s if hasattr(s, "dtype") else jax.ShapeDtypeStruct(s, F32) for s in outs]
    return pl.pallas_call(
        body,
        out_shape=shapes,
        in_specs=[pl.BlockSpec(memory_space=space)] * len(args),
        out_specs=[pl.BlockSpec(memory_space=pltpu.VMEM)] * len(outs),
        scratch_shapes=[pltpu.VMEM(s, F32) if isinstance(s, tuple) else s for s in scratch],
        name=body.__name__,
        compiler_params=pltpu.CompilerParams(vmem_limit_bytes=VMEM),
    )(*args)


def on_device(tracers, cotangent, east_vel, north_vel, sea_mask, level_count):
    n_trac, lev, rows, cols = tracers.shape
    assert (rows, cols, lev * SLOT) == (ROWS, LANES, LANES)
    n_lon, n_lat = lax.axis_size("lon"), lax.axis_size("lat")
    assert n_lat % 2 == 0
    n_pairs = (n_trac + 1) * lev + 1
    n_fields = 2 * n_trac + 3
    n_sent = -(-n_fields * RIM // SLOT)
    tile = (rows, cols)

    def swap_a(x):
        with jax.named_scope("swap_a"):
            return lax.ppermute(x, "lat", [(j, j ^ 1) for j in range(n_lat)])

    def swap_b(x):
        with jax.named_scope("swap_b"):
            return lax.ppermute(x, "lat", [(j, (((j + 1) ^ 1) - 1) % n_lat) for j in range(n_lat)])

    def shift(x, by):
        with jax.named_scope("east" if by > 0 else "west"):
            return lax.ppermute(x, "lon", [(i, (i + by) % n_lon) for i in range(n_lon)])

    args = (tracers, cotangent, east_vel, north_vel, sea_mask, level_count)
    args = [pltpu.with_memory_space_constraint(a, pltpu.HBM) for a in args]
    *args, pair_a, pair_b, to_west, to_east, edge = call(
        pack_kernel,
        [jax.ShapeDtypeStruct(a.shape, a.dtype) for a in args]
        + [(n_pairs,) + tile] * 2
        + [(n_sent,) + tile] * 2
        + [(n_fields,) + tile],
        args,
        [pltpu.SemaphoreType.DMA((len(args),))],
        pltpu.HBM,
    )
    from_west = shift(to_east, 1)
    from_east = shift(to_west, -1)
    pair_b = swap_b(pair_b)
    pair_a = swap_a(pair_a)
    corner_a, corner_b = call(corner_kernel, [(n_sent,) + tile] * 2, (from_west, from_east))
    corner_a = swap_a(corner_a)
    corner_b = swap_b(corner_b)
    outs = [tracers.shape, east_vel.shape, north_vel.shape]
    *main, edge_rim = call(
        main_kernel,
        outs + [(n_fields,) + tile],
        (*args, pair_a, pair_b),
        [(4, n_trac, lev, 2) + tile, (STEPS, 2, n_trac, lev) + tile, (len(COEFS), lev, 2) + tile],
    )
    return tuple(
        call(edge_kernel, outs, (edge, edge_rim, from_west, from_east, corner_a, corner_b, *main))
    )


def solution(mesh):
    state, flat, cell = P(None, None, "lat", "lon"), P(None, "lat", "lon"), P("lat", "lon")
    return jax.shard_map(
        on_device,
        mesh=mesh,
        in_specs=(state, state, flat, flat, cell, cell),
        out_specs=(state, flat, flat),
        check_vma=False,
    )
```

time: 70.5 us -> 17.2 us (0.24)
  the two profiles are of different devices: /device:TPU:3 before, /device:TPU:0 now
where the time goes in v1:
time: 17.2 us; the launch traced here: 17 us
  starting transfers between devices  8.63 us (50%)
  waiting for transfers between devices  3.97 us (23%)
  Pallas kernels  3.77 us (22%)
  between operations  0.68 us (4%)
    ppermute x2, starting transfers between devices, swap_b(): lax.ppermute(x, 'lat', [(j, ((j + 1 ^ 1) - 1) % n_lat) for j in range(n_l...  4.18 us
    ppermute x2, starting transfers between devices, shift(): return lax.ppermute(x, 'lon', [(i, (i + by) % n_lon) for i in range(n_lon)])  3.82 us
    pallas_call x4, Pallas kernels, call(): pl.pallas_call(body, out_shape=shapes, in_specs=[pl.BlockSpec(memory_spac...  3.77 us
    ppermute x2, waiting for transfers between devices, swap_b(): lax.ppermute(x, 'lat', [(j, ((j + 1 ^ 1) - 1) % n_lat) for j in range(n_l...  2.29 us
    ppermute x2, waiting for transfers between devices, shift(): return lax.ppermute(x, 'lon', [(i, (i + by) % n_lon) for i in range(n_lon)])  1.67 us
    ppermute x2, starting transfers between devices, swap_a(): return lax.ppermute(x, 'lat', [(j, j ^ 1) for j in range(n_lat)])  0.63 us
  transfers between devices with their start and end apart: 6, of which 2 were waited for; matrix products, arithmetic and copies ran while one was open for 0% of the time, Pallas kernels for 7%

profile of v1, /device:TPU:0, one launch (start us, length us, event | category | flops | bytes accessed | tf_op | source)
XLA Modules:
  0.0 17.0 jit_solution(10409731785239110763)
XLA Ops:
  0.6 1.2 %pack_kernel.1 = (f32[3,8,8,128]{3,2,1,0:T(8,128)S(1)}, f32[3,8,8,128]{3,2,1,0:T(8,128)S(1)}, f32[8,8,128]{2,1,0:T(8,128)S(1)}, f32[8,8,128]{2,1,0:T(8,128)S(1)}...) custom-call(f32[3,8,8,128]{3,2,1,0:T(8,128)} %refs_0_.1, ...), custom_call_target="tpu_custom_call" | custom-call | tf_op jit(solution)/shard_map/pack_kernel/pallas_call | solution.py:352
  1.8 0.6 %collective-permute-start = (f32[33,8,128]{2,1,0:T(8,128)S(1)}, f32[33,8,128]{2,1,0:T(8,128)S(1)}, u32[]{:S(2)}, u32[]{:S(2)}) collective-permute-start(f32[33,8,128]{2,1,0:T(8,128)S(1)} %get-tuple-element.27), channel_id=1, source_target_pairs={{0,1},{1,0},{2,3},{3,2},{4,5},{5,4},{6,7},{7,6},{8,9},{9,8},{10,11... | collective-permute-start | bytes 405512 | tf_op jit(solution)/shard_map/swap_a/ppermute | solution.py:375
  2.4 3.5 %collective-permute-start.1 = (f32[33,8,128]{2,1,0:T(8,128)S(1)}, f32[33,8,128]{2,1,0:T(8,128)S(1)}, u32[]{:S(2)}, u32[]{:S(2)}) collective-permute-start(f32[33,8,128]{2,1,0:T(8,128)S(1)} %get-tuple-element.28), channel_id=1, source_target_pairs={{0,7},{1,2},{2,1},{3,4},{4,3},{5,6},{6,5},{7,0},{8,15},{9,10},{10,... | collective-permute-start | bytes 405512 | tf_op jit(solution)/shard_map/swap_b/ppermute | solution.py:379
  5.9 1.6 %collective-permute-start.2 = (f32[3,8,128]{2,1,0:T(8,128)S(1)}, f32[3,8,128]{2,1,0:T(8,128)S(1)}, u32[]{:S(2)}, u32[]{:S(2)}) collective-permute-start(f32[3,8,128]{2,1,0:T(8,128)S(1)} %get-tuple-element.30), channel_id=1, source_target_pairs={{0,8},{8,16},{16,24},{24,0},{1,9},{9,17},{17,25},{25,1},{2,10},{10... | collective-permute-start | bytes 36872 | tf_op jit(solution)/shard_map/east/ppermute | solution.py:383
  7.5 2.2 %collective-permute-start.3 = (f32[3,8,128]{2,1,0:T(8,128)S(1)}, f32[3,8,128]{2,1,0:T(8,128)S(1)}, u32[]{:S(2)}, u32[]{:S(2)}) collective-permute-start(f32[3,8,128]{2,1,0:T(8,128)S(1)} %get-tuple-element.31), channel_id=1, source_target_pairs={{0,24},{8,0},{16,8},{24,16},{1,25},{9,1},{17,9},{25,17},{2,26},{10... | collective-permute-start | bytes 36872 | tf_op jit(solution)/shard_map/west/ppermute | solution.py:383
  9.8 1.7 %collective-permute-done.2.from_west = f32[3,8,128]{2,1,0:T(8,128)S(1)} collective-permute-done((f32[3,8,128]{2,1,0:T(8,128)S(1)}, f32[3,8,128]{2,1,0:T(8,128)S(1)}, u32[]{:S(2)}, u32[]{:S(2)}) %collective-permute-start.2) | collective-permute-done | bytes 12320 | tf_op jit(solution)/shard_map/east/ppermute | solution.py:383
  11.4 0.0 collective-permute-done.3.from_east
  11.5 0.1 collective-permute-start.4
  11.5 0.6 %collective-permute-start.5 = (f32[3,8,128]{2,1,0:T(8,128)S(1)}, f32[3,8,128]{2,1,0:T(8,128)S(1)}, u32[]{:S(2)}, u32[]{:S(2)}) collective-permute-start(f32[3,8,128]{2,1,0:T(8,128)S(1)} %get-tuple-element.33), channel_id=1, source_target_pairs={{0,7},{1,2},{2,1},{3,4},{4,3},{5,6},{6,5},{7,0},{8,15},{9,10},{10,... | collective-permute-start | bytes 36872 | tf_op jit(solution)/shard_map/swap_b/ppermute | solution.py:379
  12.2 0.0 collective-permute-done.pair_a
  12.2 0.0 collective-permute-done.1.pair_b
  12.2 1.1 %main_kernel.1 = (f32[3,8,8,128]{3,2,1,0:T(8,128)S(1)}, f32[8,8,128]{2,1,0:T(8,128)S(1)}, f32[8,8,128]{2,1,0:T(8,128)S(1)}, f32[9,8,128]{2,1,0:T(8,128)S(1)}) custom-call(f32[3,8,8,128]{3,2,1,0:T(8,128)S(1)} %get-tuple-element.21.trac, f32[3,8,8,128]{3,2,1,0:T(8,128)S(1)} %get-tuple-element.22.cot, f32[8,8,128]{2,1,0:T(8,128)S(1)} %get-tuple-element.23.east_vel, ...), custom_call_target="tpu_custom_call" | custom-call | tf_op jit(solution)/shard_map/main_kernel/pallas_call | solution.py:352
  13.3 0.0 collective-permute-done.4.pair_a
  13.3 2.3 %collective-permute-done.5.pair_b = f32[3,8,128]{2,1,0:T(8,128)S(1)} collective-permute-done((f32[3,8,128]{2,1,0:T(8,128)S(1)}, f32[3,8,128]{2,1,0:T(8,128)S(1)}, u32[]{:S(2)}, u32[]{:S(2)}) %collective-permute-start.5) | collective-permute-done | bytes 12320 | tf_op jit(solution)/shard_map/swap_b/ppermute | solution.py:379
  15.6 1.4 %edge_kernel.1 = (f32[3,8,8,128]{3,2,1,0:T(8,128)}, f32[8,8,128]{2,1,0:T(8,128)}, f32[8,8,128]{2,1,0:T(8,128)}) custom-call(f32[9,8,128]{2,1,0:T(8,128)S(1)} %get-tuple-element.20.edge, f32[9,8,128]{2,1,0:T(8,128)S(1)} %get-tuple-element.29.edge_rim, f32[3,8,128]{2,1,0:T(8,128)S(1)} %collective-permute-done.2.from_west, ...), custom_call_target="tpu_custom_call" | custom-call | tf_op jit(solution)/shard_map/edge_kernel/pallas_call | solution.py:352
  (1 shorter events, 0.0 us)
Async XLA Ops:
  1.8 10.3 %collective-permute-start = (f32[33,8,128]{2,1,0:T(8,128)S(1)}, f32[33,8,128]{2,1,0:T(8,128)S(1)}, u32[]{:S(2)}, u32[]{:S(2)}) collective-permute-start(f32[33,8,128]{2,1,0:T(8,128)S(1)} %get-tuple-element.27), channel_id=1, source_target_pairs={{0,1},{1,0},{2,3},{3,2},{4,5},{5,4},{6,7},{7,6},{8,9},{9,8},{10,11... | collective-permute-start | bytes 405512 | tf_op jit(solution)/shard_map/swap_a/ppermute | solution.py:375
  2.4 9.8 %collective-permute-start.1 = (f32[33,8,128]{2,1,0:T(8,128)S(1)}, f32[33,8,128]{2,1,0:T(8,128)S(1)}, u32[]{:S(2)}, u32[]{:S(2)}) collective-permute-start(f32[33,8,128]{2,1,0:T(8,128)S(1)} %get-tuple-element.28), channel_id=1, source_target_pairs={{0,7},{1,2},{2,1},{3,4},{4,3},{5,6},{6,5},{7,0},{8,15},{9,10},{10,... | collective-permute-start | bytes 405512 | tf_op jit(solution)/shard_map/swap_b/ppermute | solution.py:379
  5.9 5.5 %collective-permute-start.2 = (f32[3,8,128]{2,1,0:T(8,128)S(1)}, f32[3,8,128]{2,1,0:T(8,128)S(1)}, u32[]{:S(2)}, u32[]{:S(2)}) collective-permute-start(f32[3,8,128]{2,1,0:T(8,128)S(1)} %get-tuple-element.30), channel_id=1, source_target_pairs={{0,8},{8,16},{16,24},{24,0},{1,9},{9,17},{17,25},{25,1},{2,10},{10... | collective-permute-start | bytes 36872 | tf_op jit(solution)/shard_map/east/ppermute | solution.py:383
  7.5 3.9 %collective-permute-start.3 = (f32[3,8,128]{2,1,0:T(8,128)S(1)}, f32[3,8,128]{2,1,0:T(8,128)S(1)}, u32[]{:S(2)}, u32[]{:S(2)}) collective-permute-start(f32[3,8,128]{2,1,0:T(8,128)S(1)} %get-tuple-element.31), channel_id=1, source_target_pairs={{0,24},{8,0},{16,8},{24,16},{1,25},{9,1},{17,9},{25,17},{2,26},{10... | collective-permute-start | bytes 36872 | tf_op jit(solution)/shard_map/west/ppermute | solution.py:383
  11.5 1.9 %collective-permute-start.4 = (f32[3,8,128]{2,1,0:T(8,128)S(1)}, f32[3,8,128]{2,1,0:T(8,128)S(1)}, u32[]{:S(2)}, u32[]{:S(2)}) collective-permute-start(f32[3,8,128]{2,1,0:T(8,128)S(1)} %get-tuple-element.32), channel_id=1, source_target_pairs={{0,1},{1,0},{2,3},{3,2},{4,5},{5,4},{6,7},{7,6},{8,9},{9,8},{10,11... | collective-permute-start | bytes 36872 | tf_op jit(solution)/shard_map/swap_a/ppermute | solution.py:375
  11.5 4.1 %collective-permute-start.5 = (f32[3,8,128]{2,1,0:T(8,128)S(1)}, f32[3,8,128]{2,1,0:T(8,128)S(1)}, u32[]{:S(2)}, u32[]{:S(2)}) collective-permute-start(f32[3,8,128]{2,1,0:T(8,128)S(1)} %get-tuple-element.33), channel_id=1, source_target_pairs={{0,7},{1,2},{2,1},{3,4},{4,3},{5,6},{6,5},{7,0},{8,15},{9,10},{10,... | collective-permute-start | bytes 36872 | tf_op jit(solution)/shard_map/swap_b/ppermute | solution.py:379

commit v2 on v1

--- a/solution.py
+++ b/solution.py
@@ -4,6 +4,7 @@
 from jax.experimental import pallas as pl
 from jax.experimental.pallas import tpu as pltpu
 from jax.sharding import PartitionSpec as P
+
 
 STEPS = 4
 HORIZ = 0.22
@@ -355,12 +356,11 @@
         in_specs=[pl.BlockSpec(memory_space=space)] * len(args),
         out_specs=[pl.BlockSpec(memory_space=pltpu.VMEM)] * len(outs),
         scratch_shapes=[pltpu.VMEM(s, F32) if isinstance(s, tuple) else s for s in scratch],
-        name=body.__name__,
         compiler_params=pltpu.CompilerParams(vmem_limit_bytes=VMEM),
     )(*args)
 
 
-def on_device(tracers, cotangent, east_vel, north_vel, sea_mask, level_count):
+def adjoint(tracers, cotangent, east_vel, north_vel, sea_mask, level_count):
     n_trac, lev, rows, cols = tracers.shape
     assert (rows, cols, lev * SLOT) == (ROWS, LANES, LANES)
     n_lon, n_lat = lax.axis_size("lon"), lax.axis_size("lat")
@@ -371,16 +371,19 @@
     tile = (rows, cols)
 
     def swap_a(x):
-        with jax.named_scope("swap_a"):
-            return lax.ppermute(x, "lat", [(j, j ^ 1) for j in range(n_lat)])
+        return lax.ppermute(x, "lat", [(j, j ^ 1) for j in range(n_lat)])
 
     def swap_b(x):
-        with jax.named_scope("swap_b"):
-            return lax.ppermute(x, "lat", [(j, (((j + 1) ^ 1) - 1) % n_lat) for j in range(n_lat)])
+        pairs = []
+        for i in range(n_lon):
+            for j in range(n_lat):
+                end = j in (0, n_lat - 1)
+                to = (i ^ 1, j) if end else (i, ((j + 1) ^ 1) - 1)
+                pairs.append((i * n_lat + j, to[0] * n_lat + to[1]))
+        return lax.ppermute(x, ("lon", "lat"), pairs)
 
     def shift(x, by):
-        with jax.named_scope("east" if by > 0 else "west"):
-            return lax.ppermute(x, "lon", [(i, (i + by) % n_lon) for i in range(n_lon)])
+        return lax.ppermute(x, "lon", [(i, (i + by) % n_lon) for i in range(n_lon)])
 
     args = (tracers, cotangent, east_vel, north_vel, sea_mask, level_count)
     args = [pltpu.with_memory_space_constraint(a, pltpu.HBM) for a in args]
@@ -416,7 +419,7 @@
 def solution(mesh):
     state, flat, cell = P(None, None, "lat", "lon"), P(None, "lat", "lon"), P("lat", "lon")
     return jax.shard_map(
-        on_device,
+        adjoint,
         mesh=mesh,
         in_specs=(state, state, flat, flat, cell, cell),
         out_specs=(state, flat, flat),

time: 17.2 us -> 16.2 us (0.942)
  waiting for transfers between devices: 3.97 us -> 3.33 us
  starting transfers between devices: 8.63 us -> 8.27 us
    ppermute x2, waiting for transfers between devices: 2.29 us -> 1.42 us  [swap_b(): return lax.ppermute(x, ('lon', 'lat'), pairs)]
    ppermute x2, starting transfers between devices: 4.18 us -> 3.82 us  [swap_b(): return lax.ppermute(x, ('lon', 'lat'), pairs)]
    ppermute x2, waiting for transfers between devices: 1.67 us -> 1.9 us  [shift(): return lax.ppermute(x, 'lon', [(i, (i + by) % n_lon) for i in range(n_lon)])]
where the time goes in v2:
time: 16.2 us; the launch traced here: 16 us
  starting transfers between devices  8.27 us (51%)
  Pallas kernels  3.77 us (23%)
  waiting for transfers between devices  3.33 us (21%)
  between operations  0.68 us (4%)
    ppermute x2, starting transfers between devices, shift(): return lax.ppermute(x, 'lon', [(i, (i + by) % n_lon) for i in range(n_lon)])  3.82 us
    ppermute x2, starting transfers between devices, swap_b(): return lax.ppermute(x, ('lon', 'lat'), pairs)  3.82 us
    pallas_call x4, Pallas kernels, call(): pl.pallas_call(body, out_shape=shapes, in_specs=[pl.BlockSpec(memory_spac...  3.77 us
    ppermute x2, waiting for transfers between devices, shift(): return lax.ppermute(x, 'lon', [(i, (i + by) % n_lon) for i in range(n_lon)])  1.9 us
    ppermute x2, waiting for transfers between devices, swap_b(): return lax.ppermute(x, ('lon', 'lat'), pairs)  1.42 us
    ppermute x2, starting transfers between devices, swap_a(): return lax.ppermute(x, 'lat', [(j, j ^ 1) for j in range(n_lat)])  0.63 us
  transfers between devices with their start and end apart: 6, of which 2 were waited for; matrix products, arithmetic and copies ran while one was open for 0% of the time, Pallas kernels for 7%

profile of v2, /device:TPU:0, one launch (start us, length us, event | category | flops | bytes accessed | tf_op | source)
XLA Modules:
  0.0 16.0 jit_solution(11015267442467266704)
XLA Ops:
  0.6 1.2 %shard_map.85 = (f32[3,8,8,128]{3,2,1,0:T(8,128)S(1)}, f32[3,8,8,128]{3,2,1,0:T(8,128)S(1)}, f32[8,8,128]{2,1,0:T(8,128)S(1)}, f32[8,8,128]{2,1,0:T(8,128)S(1)},...) custom-call(f32[3,8,8,128]{3,2,1,0:T(8,128)} %refs_0_.1, ...), custom_call_target="tpu_custom_call" | custom-call | tf_op jit(solution)/shard_map/pallas_call | solution.py:353
  1.8 0.6 %collective-permute-start = (f32[33,8,128]{2,1,0:T(8,128)S(1)}, f32[33,8,128]{2,1,0:T(8,128)S(1)}, u32[]{:S(2)}, u32[]{:S(2)}) collective-permute-start(f32[33,8,128]{2,1,0:T(8,128)S(1)} %get-tuple-element.27), channel_id=1, source_target_pairs={{0,1},{1,0},{2,3},{3,2},{4,5},{5,4},{6,7},{7,6},{8,9},{9,8},{10,11... | collective-permute-start | bytes 405512 | tf_op jit(solution)/shard_map/ppermute | solution.py:374
  2.4 2.6 %collective-permute-start.1 = (f32[33,8,128]{2,1,0:T(8,128)S(1)}, f32[33,8,128]{2,1,0:T(8,128)S(1)}, u32[]{:S(2)}, u32[]{:S(2)}) collective-permute-start(f32[33,8,128]{2,1,0:T(8,128)S(1)} %get-tuple-element.28), channel_id=1, source_target_pairs={{0,8},{1,2},{2,1},{3,4},{4,3},{5,6},{6,5},{7,15},{8,0},{9,10},{10,... | collective-permute-start | bytes 405512 | tf_op jit(solution)/shard_map/ppermute | solution.py:383
  5.0 0.1 collective-permute-start.2
  5.1 3.8 %collective-permute-start.3 = (f32[3,8,128]{2,1,0:T(8,128)S(1)}, f32[3,8,128]{2,1,0:T(8,128)S(1)}, u32[]{:S(2)}, u32[]{:S(2)}) collective-permute-start(f32[3,8,128]{2,1,0:T(8,128)S(1)} %get-tuple-element.31), channel_id=1, source_target_pairs={{0,24},{8,0},{16,8},{24,16},{1,25},{9,1},{17,9},{25,17},{2,26},{10... | collective-permute-start | bytes 36872 | tf_op jit(solution)/shard_map/ppermute | solution.py:386
  8.9 1.9 %collective-permute-done.2.from_west = f32[3,8,128]{2,1,0:T(8,128)S(1)} collective-permute-done((f32[3,8,128]{2,1,0:T(8,128)S(1)}, f32[3,8,128]{2,1,0:T(8,128)S(1)}, u32[]{:S(2)}, u32[]{:S(2)}) %collective-permute-start.2) | collective-permute-done | bytes 12320 | tf_op jit(solution)/shard_map/ppermute | solution.py:386
  10.8 0.0 collective-permute-done.3.from_east
  10.8 0.1 collective-permute-start.4
  10.9 1.2 %collective-permute-start.5 = (f32[3,8,128]{2,1,0:T(8,128)S(1)}, f32[3,8,128]{2,1,0:T(8,128)S(1)}, u32[]{:S(2)}, u32[]{:S(2)}) collective-permute-start(f32[3,8,128]{2,1,0:T(8,128)S(1)} %get-tuple-element.33), channel_id=1, source_target_pairs={{0,8},{1,2},{2,1},{3,4},{4,3},{5,6},{6,5},{7,15},{8,0},{9,10},{10,... | collective-permute-start | bytes 36872 | tf_op jit(solution)/shard_map/ppermute | solution.py:383
  12.0 0.0 collective-permute-done.pair_a
  12.0 0.0 collective-permute-done.1.pair_b
  12.0 1.1 %shard_map.86 = (f32[3,8,8,128]{3,2,1,0:T(8,128)S(1)}, f32[8,8,128]{2,1,0:T(8,128)S(1)}, f32[8,8,128]{2,1,0:T(8,128)S(1)}, f32[9,8,128]{2,1,0:T(8,128)S(1)}) custom-call(f32[3,8,8,128]{3,2,1,0:T(8,128)S(1)} %get-tuple-element.21.trac, f32[3,8,8,128]{3,2,1,0:T(8,128)S(1)} %get-tuple-element.22.cot, f32[8,8,128]{2,1,0:T(8,128)S(1)} %get-tuple-element.23.east_vel, ...), custom_call_target="tpu_custom_call" | custom-call | tf_op jit(solution)/shard_map/pallas_call | solution.py:353
  13.2 0.0 collective-permute-done.4.pair_a
  13.2 1.4 %collective-permute-done.5.pair_b = f32[3,8,128]{2,1,0:T(8,128)S(1)} collective-permute-done((f32[3,8,128]{2,1,0:T(8,128)S(1)}, f32[3,8,128]{2,1,0:T(8,128)S(1)}, u32[]{:S(2)}, u32[]{:S(2)}) %collective-permute-start.5) | collective-permute-done | bytes 12320 | tf_op jit(solution)/shard_map/ppermute | solution.py:383
  14.6 1.4 %shard_map.88 = (f32[3,8,8,128]{3,2,1,0:T(8,128)}, f32[8,8,128]{2,1,0:T(8,128)}, f32[8,8,128]{2,1,0:T(8,128)}) custom-call(f32[9,8,128]{2,1,0:T(8,128)S(1)} %get-tuple-element.20.edge, f32[9,8,128]{2,1,0:T(8,128)S(1)} %get-tuple-element.29.edge_rim, f32[3,8,128]{2,1,0:T(8,128)S(1)} %collective-permute-done.2.from_west, ...), custom_call_target="tpu_custom_call" | custom-call | tf_op jit(solution)/shard_map/pallas_call | solution.py:353
  (1 shorter events, 0.0 us)
Async XLA Ops:
  1.8 10.2 %collective-permute-start = (f32[33,8,128]{2,1,0:T(8,128)S(1)}, f32[33,8,128]{2,1,0:T(8,128)S(1)}, u32[]{:S(2)}, u32[]{:S(2)}) collective-permute-start(f32[33,8,128]{2,1,0:T(8,128)S(1)} %get-tuple-element.27), channel_id=1, source_target_pairs={{0,1},{1,0},{2,3},{3,2},{4,5},{5,4},{6,7},{7,6},{8,9},{9,8},{10,11... | collective-permute-start | bytes 405512 | tf_op jit(solution)/shard_map/ppermute | solution.py:374
  2.4 9.6 %collective-permute-start.1 = (f32[33,8,128]{2,1,0:T(8,128)S(1)}, f32[33,8,128]{2,1,0:T(8,128)S(1)}, u32[]{:S(2)}, u32[]{:S(2)}) collective-permute-start(f32[33,8,128]{2,1,0:T(8,128)S(1)} %get-tuple-element.28), channel_id=1, source_target_pairs={{0,8},{1,2},{2,1},{3,4},{4,3},{5,6},{6,5},{7,15},{8,0},{9,10},{10,... | collective-permute-start | bytes 405512 | tf_op jit(solution)/shard_map/ppermute | solution.py:383
  5.0 5.7 %collective-permute-start.2 = (f32[3,8,128]{2,1,0:T(8,128)S(1)}, f32[3,8,128]{2,1,0:T(8,128)S(1)}, u32[]{:S(2)}, u32[]{:S(2)}) collective-permute-start(f32[3,8,128]{2,1,0:T(8,128)S(1)} %get-tuple-element.30), channel_id=1, source_target_pairs={{0,8},{8,16},{16,24},{24,0},{1,9},{9,17},{17,25},{25,1},{2,10},{10... | collective-permute-start | bytes 36872 | tf_op jit(solution)/shard_map/ppermute | solution.py:386
  5.1 5.7 %collective-permute-start.3 = (f32[3,8,128]{2,1,0:T(8,128)S(1)}, f32[3,8,128]{2,1,0:T(8,128)S(1)}, u32[]{:S(2)}, u32[]{:S(2)}) collective-permute-start(f32[3,8,128]{2,1,0:T(8,128)S(1)} %get-tuple-element.31), channel_id=1, source_target_pairs={{0,24},{8,0},{16,8},{24,16},{1,25},{9,1},{17,9},{25,17},{2,26},{10... | collective-permute-start | bytes 36872 | tf_op jit(solution)/shard_map/ppermute | solution.py:386
  10.8 2.4 %collective-permute-start.4 = (f32[3,8,128]{2,1,0:T(8,128)S(1)}, f32[3,8,128]{2,1,0:T(8,128)S(1)}, u32[]{:S(2)}, u32[]{:S(2)}) collective-permute-start(f32[3,8,128]{2,1,0:T(8,128)S(1)} %get-tuple-element.32), channel_id=1, source_target_pairs={{0,1},{1,0},{2,3},{3,2},{4,5},{5,4},{6,7},{7,6},{8,9},{9,8},{10,11... | collective-permute-start | bytes 36872 | tf_op jit(solution)/shard_map/ppermute | solution.py:374
  10.9 3.8 %collective-permute-start.5 = (f32[3,8,128]{2,1,0:T(8,128)S(1)}, f32[3,8,128]{2,1,0:T(8,128)S(1)}, u32[]{:S(2)}, u32[]{:S(2)}) collective-permute-start(f32[3,8,128]{2,1,0:T(8,128)S(1)} %get-tuple-element.33), channel_id=1, source_target_pairs={{0,8},{1,2},{2,1},{3,4},{4,3},{5,6},{6,5},{7,15},{8,0},{9,10},{10,... | collective-permute-start | bytes 36872 | tf_op jit(solution)/shard_map/ppermute | solution.py:383

commit v3 on v2

v3 whole, which is shorter than its diff:
```python
import jax
import jax.numpy as jnp
from jax import lax
from jax.experimental import pallas as pl
from jax.experimental.pallas import tpu as pltpu
from jax.sharding import PartitionSpec as P


STEPS = 4
HORIZ = 0.22
VERT = 0.05

ROWS = 8
LANES = 128
RIM = 4
SLOT = 16
F32 = jnp.float32
VMEM = 8 << 20


def iota(axis):
    return lax.broadcasted_iota(jnp.int32, (ROWS, LANES), axis)


def lane_roll(x, shift):
    shift %= LANES
    return x if shift == 0 else pltpu.roll(x, shift, 1)


def row_roll(x, shift):
    return pltpu.roll(x, shift % ROWS, 0)


def east(x):
    return lane_roll(x, -1)


def west(x):
    return lane_roll(x, 1)


def north(own, rim, last):
    a, b = row_roll(own, -1), row_roll(rim, -1)
    return jnp.where(last, b, a), jnp.where(last, a, b)


def south(own, rim, first):
    a, b = row_roll(own, 1), row_roll(rim, 1)
    return jnp.where(first, b, a), jnp.where(first, a, b)


def odd_row():
    return lax.rem(lax.axis_index("lat"), 2)


def wet_count(mask, count):
    return jnp.where(mask == 1, count, 0).astype(F32)


def edge_of(planes):
    slot = iota(1) // SLOT
    out = None
    for k, plane in enumerate(planes):
        moved = lane_roll(plane, SLOT * k + SLOT // 2)
        out = moved if out is None else jnp.where(slot == k, moved, out)
    return out


def inside_rows(rim):
    place, total = lax.axis_index("lat"), lax.axis_size("lat")
    sub = iota(0)
    keep = ((sub >= RIM) | (place < total - 1)) & ((sub < RIM) | (place > 0))
    return jnp.where(keep, rim, 0.0)


def pack_kernel(*refs):
    args, here, (pair_a, pair_b, to_west, to_east, edge, sems) = refs[:6], refs[6:12], refs[12:]
    copies = [pltpu.make_async_copy(a, b, sems.at[i]) for i, (a, b) in enumerate(zip(args, here))]
    for copy in copies:
        copy.start()
    for copy in copies:
        copy.wait()
    trac, cot, east_vel, north_vel, mask, count = here
    n_trac, lev = trac.shape[:2]
    upper = (iota(0) // RIM) != odd_row()

    def pair(index, p, q):
        q = row_roll(q, RIM)
        pair_a[index] = jnp.where(upper, p, q)
        pair_b[index] = jnp.where(upper, q, p)

    for t in range(n_trac):
        for k in range(lev):
            pair(t * lev + k, trac[t, k], cot[t, k])
    for k in range(lev):
        pair(n_trac * lev + k, east_vel[k], north_vel[k])
    wet = wet_count(mask[...], count[...])
    pair_a[(n_trac + 1) * lev] = wet
    pair_b[(n_trac + 1) * lev] = wet

    fields = [[trac[t, k] for k in range(lev)] for t in range(n_trac)]
    fields += [[cot[t, k] for k in range(lev)] for t in range(n_trac)]
    fields += [[ref[k] for k in range(lev)] for ref in (east_vel, north_vel)]
    fields += [[wet] * lev]
    quarter = (iota(1) % SLOT) // RIM
    west_out, east_out = {}, {}
    for f, planes in enumerate(fields):
        e = edge_of(planes)
        edge[f] = e
        d, g = divmod(f, SLOT // RIM)
        if f == len(fields) - 1 and g == 0:
            west_out[d] = east_out[d] = e
            continue
        moved = lane_roll(e, RIM * g - 8)
        if g == 0:
            west_out[d] = east_out[d] = moved
        else:
            west_out[d] = jnp.where(quarter == g, moved, west_out[d])
            east_out[d] = jnp.where(quarter == g - 1, moved, east_out[d])
    for d in west_out:
        to_west[d] = west_out[d]
        to_east[d] = east_out[d]


def corner_kernel(from_west, from_east, pair_a, pair_b):
    upper = (iota(0) // RIM) != odd_row()
    for d in range(from_west.shape[0]):
        p, q = from_west[d], row_roll(from_east[d], RIM)
        pair_a[d] = jnp.where(upper, p, q)
        pair_b[d] = jnp.where(upper, q, p)


def unpair(a, b):
    from_a = (iota(0) // RIM) == odd_row()
    return jnp.where(from_a, a, b), row_roll(jnp.where(from_a, b, a), RIM)


def velocity_terms(wet, east_wet, north_wet, u, v):
    east_open, north_open = wet * east_wet, wet * north_wet
    hu, hv = 0.5 * u, 0.5 * v
    p, q = east_open * (hu + HORIZ), east_open * (HORIZ - hu)
    r, s = north_open * (hv + HORIZ), north_open * (HORIZ - hv)
    return dict(east_open=east_open, north_open=north_open, p=p, q=q, r=r, s=s, pw=west(p), qw=west(q))


def finish(c, wet, rs, ss, wet_up, wet_down):
    c["rs"], c["ss"] = rs, ss
    centre = wet - ((c["p"] + c["qw"]) + (c["r"] + ss))
    for side, other in (("up", wet_up), ("down", wet_down)):
        if other is not None:
            c[side] = (VERT * wet) * other
            centre = centre - c[side]
    c["centre"] = centre
    return c


def coefficients(wet, wet_up, wet_down, u, v):
    sub = iota(0)
    first, last = sub == 0, sub == ROWS - 1
    north_wet = north(*wet, last)
    out = [velocity_terms(wet[h], east(wet[h]), north_wet[h], u[h], v[h]) for h in range(2)]
    rs, ss = (south(out[0][x], out[1][x], first) for x in "rs")
    for h in range(2):
        finish(out[h], wet[h], rs[h], ss[h], wet_up and wet_up[h], wet_down and wet_down[h])
    return out


FORWARD = ("q", "pw", "s", "rs")
BACKWARD = ("p", "qw", "r", "ss")
COEFS = ("centre", "p", "q", "pw", "qw", "r", "s", "rs", "ss", "up", "down", "east_open", "north_open")


def combine(coef, names, x, e, w, n, s, up, down):
    out = (coef("centre") * x + coef(names[0]) * e) + (coef(names[1]) * w + coef(names[2]) * n)
    out = out + coef(names[3]) * s
    if up is not None:
        out = out + coef("up") * up
    if down is not None:
        out = out + coef("down") * down
    return out


def add(total, term):
    return term if total is None else total + term


def packed_edges(pairs, n_trac, lev):
    groups = [[pairs[i * lev + k] for k in range(lev)] for i in range(n_trac + 1)]
    return [edge_of(g) for g in groups] + [edge_of([pairs[(n_trac + 1) * lev]] * lev)]


def near_kernel(trac, cot, east_vel, north_vel, mask, count, pair_a, adj_t, adj_e, adj_n, past, past_adj, edge_a, rims, sums, coef):
    n_trac, lev = trac.shape[:2]
    sub = iota(0)
    first, last = sub == 0, sub == ROWS - 1
    for i, e in enumerate(packed_edges(pair_a, n_trac, lev)):
        edge_a[i] = e

    def rim(index):
        x = pair_a[index]
        return x, row_roll(x, RIM)

    for t in range(n_trac):
        for k in range(lev):
            rims[0, t, k], rims[2, t, k] = rim(t * lev + k)
    own_side = (sub // RIM) == odd_row()
    count_own = wet_count(mask[...], count[...])
    count_rim = jnp.where(own_side, pair_a[(n_trac + 1) * lev], 0.0)
    wet = [tuple(jnp.where(x > k, 1.0, 0.0) for x in (count_own, count_rim)) for k in range(lev)]
    for k in range(lev):
        u_rim, v_rim = rim(n_trac * lev + k)
        made = coefficients(
            wet[k],
            wet[k + 1] if k + 1 < lev else None,
            wet[k - 1] if k else None,
            (east_vel[k], u_rim),
            (north_vel[k], v_rim),
        )
        for h in range(2):
            for name, value in made[h].items():
                coef[COEFS.index(name), k, h] = value

    def states(own, buf):
        return lambda t, k: (own[t, k], rims[buf, t, k])

    def neighbours(pair):
        own, out = pair
        n, s = north(own, out, last), south(own, out, first)
        return (own, out), (east(own), east(out)), (west(own), west(out)), n, s

    def apply(get, k, t, about, names, h):
        x, e, w, n, s = about
        up = get(t, k + 1)[h] if k + 1 < lev else None
        down = get(t, k - 1)[h] if k else None
        return combine(lambda name: coef[COEFS.index(name), k, h], names, x[h], e[h], w[h], n[h], s[h], up, down)

    for step in range(STEPS):
        get = states(past.at[step - 1] if step else trac, step % 2)
        for k in range(lev):
            for t in range(n_trac):
                if step < STEPS - 1:
                    about = neighbours(get(t, k))
                    past[step, t, k] = apply(get, k, t, about, FORWARD, 0)
                    rims[(step + 1) % 2, t, k] = apply(get, k, t, about, FORWARD, 1)
                    x, e, n = about[0][0], about[1][0], about[3][0]
                else:
                    x, out = get(t, k)
                    e, n = east(x), north(x, out, last)[0]
                sums[step, 0, t, k] = x + e
                sums[step, 1, t, k] = x + n
    for done, step in enumerate(reversed(range(STEPS))):
        get = states(past_adj.at[done - 1] if done else cot, 2 + done % 2)
        for k in range(lev):
            acc_e = acc_n = None
            for t in range(n_trac):
                about = neighbours(get(t, k))
                new = apply(get, k, t, about, BACKWARD, 0)
                if step:
                    past_adj[done, t, k] = new
                    rims[2 + (done + 1) % 2, t, k] = apply(get, k, t, about, BACKWARD, 1)
                else:
                    adj_t[t, k] = new
                x, e, n = about[0][0], about[1][0], about[3][0]
                acc_e = add(acc_e, sums[step, 0, t, k] * (e - x))
                acc_n = add(acc_n, sums[step, 1, t, k] * (n - x))
            if done:
                acc_e, acc_n = acc_e + adj_e[k], acc_n + adj_n[k]
            if step == 0:
                acc_e = acc_e * (0.5 * coef[COEFS.index("east_open"), k, 0])
                acc_n = acc_n * (0.5 * coef[COEFS.index("north_open"), k, 0])
            adj_e[k] = acc_e
            adj_n[k] = acc_n


class Far:
    def __init__(self, args, pair_b, past, past_adj, state, sums, coef, acc):
        self.trac, self.cot, east_vel, north_vel, mask, count = args
        self.past, self.past_adj, self.state, self.sums, self.coef, self.acc = past, past_adj, state, sums, coef, acc
        n_trac, lev = self.n_trac, self.lev = self.trac.shape[:2]
        sub = iota(0)
        self.first, self.last = sub == 0, sub == ROWS - 1
        self.rim = (sub // RIM) == odd_row()

        def both(index, p, q):
            x = pair_b[index]
            return self.join(row_roll(x, RIM), p), self.join(x, q)

        for t in range(n_trac):
            for k in range(lev):
                state[0, t, k], state[2, t, k] = both(t * lev + k, self.trac[t, k], self.cot[t, k])
        place = lax.axis_index("lat")
        outside = (place == 0) | (place == lax.axis_size("lat") - 1)
        count_own = wet_count(mask[...], count[...])
        count_rim = row_roll(pair_b[(n_trac + 1) * lev], RIM)
        count_far = self.join(jnp.where(outside, jnp.zeros_like(count_rim), count_rim), count_own)
        own = [jnp.where(count_own > k, 1.0, 0.0) for k in range(lev)]
        far = [jnp.where(count_far > k, 1.0, 0.0) for k in range(lev)]
        for k in range(lev):
            u, v = both(n_trac * lev + k, east_vel[k], north_vel[k])
            beyond = velocity_terms(own[k], own[k], row_roll(own[k], -1), north_vel[k], north_vel[k])
            made = velocity_terms(far[k], east(far[k]), self.north(far[k], own[k]), u, v)
            rs, ss = (self.south(made[x], beyond[x]) for x in "rs")
            finish(made, far[k], rs, ss, far[k + 1] if k + 1 < lev else None, far[k - 1] if k else None)
            for name, value in made.items():
                coef[COEFS.index(name), k] = value

    def join(self, rim, own):
        return jnp.where(self.rim, rim, row_roll(own, RIM))

    def north(self, x, beyond):
        return jnp.where(self.last, row_roll(beyond, 3), row_roll(x, -1))

    def south(self, x, beyond):
        return jnp.where(self.first, row_roll(beyond, -3), row_roll(x, 1))

    def apply(self, buf, t, k, about, names):
        up = self.state[buf, t, k + 1] if k + 1 < self.lev else None
        down = self.state[buf, t, k - 1] if k else None
        return combine(lambda name: self.coef[COEFS.index(name), k], names, *about, up, down)

    def forward(self, step):
        src, dst = step % 2, (step + 1) % 2
        own = self.past.at[step - 1] if step else self.trac
        for k in range(self.lev):
            for t in range(self.n_trac):
                x, beyond = self.state[src, t, k], own[t, k]
                e, n = east(x), self.north(x, beyond)
                self.sums[step, 0, t, k] = x + e
                self.sums[step, 1, t, k] = x + n
                if step < STEPS - 1:
                    about = x, e, west(x), n, self.south(x, beyond)
                    self.state[dst, t, k] = self.apply(src, t, k, about, FORWARD)

    def backward(self, done):
        step = STEPS - 1 - done
        src, dst = 2 + done % 2, 2 + (done + 1) % 2
        own = self.past_adj.at[done - 1] if done else self.cot
        for k in range(self.lev):
            acc_e = acc_n = None
            for t in range(self.n_trac):
                x, beyond = self.state[src, t, k], own[t, k]
                e, n = east(x), self.north(x, beyond)
                about = x, e, west(x), n, self.south(x, beyond)
                self.state[dst, t, k] = self.apply(src, t, k, about, BACKWARD)
                acc_e = add(acc_e, self.sums[step, 0, t, k] * (e - x))
                acc_n = add(acc_n, self.sums[step, 1, t, k] * (n - x))
            if done:
                acc_e, acc_n = acc_e + self.acc[0, k], acc_n + self.acc[1, k]
            self.acc[0, k], self.acc[1, k] = acc_e, acc_n

    def merged(self, t, k, near):
        return jnp.where(self.rim, row_roll(self.state[2 + STEPS % 2, t, k], RIM), near)

    def merged_gradient(self, i, k, near):
        opened = self.coef[COEFS.index(("east_open", "north_open")[i]), k]
        return jnp.where(self.rim, row_roll(self.acc[i, k] * (0.5 * opened), RIM), near)


class Strip:
    def __init__(self, side, n_trac, lev, edge, rims, sent, corners):
        self.n_trac = n_trac
        n_fields = edge.shape[0]
        sub, lane = iota(0), iota(1)
        self.first, self.last = sub == 0, sub == ROWS - 1
        level = lane // SLOT
        from_side = (lane % SLOT) // RIM == 1 + side

        def field(f):
            d, g = divmod(f, SLOT // RIM)
            shift = 0 if f == n_fields - 1 and g == 0 else 8 - RIM * g
            own = jnp.where(from_side, lane_roll(sent[d], shift), edge[f])
            rim = jnp.where(from_side, lane_roll(corners[d], shift), rims[f])
            return own, rim

        own, rim = field(n_fields - 1)
        levels = level.astype(F32)
        wet = tuple(jnp.where(x > levels, 1.0, 0.0) for x in (own, inside_rows(rim)))
        up = tuple(jnp.where(level < lev - 1, lane_roll(x, -SLOT), 0.0) for x in wet)
        down = tuple(jnp.where(level > 0, lane_roll(x, SLOT), 0.0) for x in wet)
        self.made = coefficients(wet, up, down, field(2 * n_trac), field(2 * n_trac + 1))
        self.state = [field(t) for t in range(n_trac)]
        self.lam = [field(n_trac + t) for t in range(n_trac)]
        self.sums, self.acc_e, self.acc_n = [], None, None

    def near(self, x):
        n, s = north(*x, self.last), south(*x, self.first)
        return x, tuple(map(east, x)), tuple(map(west, x)), n, s

    def apply(self, about, names, halves):
        x, e, w, n, s = about
        return tuple(
            combine(self.made[h].__getitem__, names, x[h], e[h], w[h], n[h], s[h], lane_roll(x[h], -SLOT), lane_roll(x[h], SLOT))
            for h in halves
        )

    def forward(self, step):
        about = [self.near(x) for x in self.state]
        self.sums.append([(a[0][0] + a[1][0], a[0][0] + a[3][0]) for a in about])
        if step < STEPS - 1:
            self.state = [self.apply(a, FORWARD, (0, 1)) for a in about]

    def backward(self, done):
        step = STEPS - 1 - done
        about = [self.near(x) for x in self.lam]
        for (sum_e, sum_n), a in zip(self.sums[step], about):
            x, e, n = a[0][0], a[1][0], a[3][0]
            self.acc_e = add(self.acc_e, sum_e * (e - x))
            self.acc_n = add(self.acc_n, sum_n * (n - x))
        self.lam = [self.apply(a, BACKWARD, (0, 1) if step else (0,)) for a in about]

    def gradients(self):
        own = self.made[0]
        return self.acc_e * (0.5 * own["east_open"]), self.acc_n * (0.5 * own["north_open"])


def far_kernel(*refs):
    args, refs = refs[:6], refs[6:]
    pair_b, near_t, near_e, near_n, past, past_adj, edge_a = refs[:7]
    adj_t, adj_e, adj_n, edge_rim, state, sums, coef, acc = refs[7:]
    n_trac, lev = near_t.shape[:2]

    for i, b in enumerate(packed_edges(pair_b, n_trac, lev)):
        p, q = unpair(edge_a[i], b)
        if i < n_trac:
            edge_rim[i], edge_rim[n_trac + i] = p, q
        elif i == n_trac:
            edge_rim[2 * n_trac], edge_rim[2 * n_trac + 1] = p, q
        else:
            edge_rim[2 * n_trac + 2] = p
    far = Far(args, pair_b, past, past_adj, state, sums, coef, acc)
    for step in range(STEPS):
        far.forward(step)
    for done in range(STEPS):
        far.backward(done)
    for k in range(lev):
        for t in range(n_trac):
            adj_t[t, k] = far.merged(t, k, near_t[t, k])
        adj_e[k] = far.merged_gradient(0, k, near_e[k])
        adj_n[k] = far.merged_gradient(1, k, near_n[k])


def edge_kernel(edge, edge_rim, from_west, from_east, corner_a, corner_b, main_t, main_e, main_n, adj_t, adj_e, adj_n):
    n_trac, lev = main_t.shape[:2]
    corners = [unpair(corner_a[d], corner_b[d]) for d in range(from_west.shape[0])]
    strips = [
        Strip(side, n_trac, lev, edge, edge_rim, sent, [c[side] for c in corners])
        for side, sent in enumerate((from_west, from_east))
    ]
    for step in range(STEPS):
        for part in strips:
            part.forward(step)
    for done in range(STEPS):
        for part in strips:
            part.backward(done)

    lane = iota(1)
    at_west = (lane % SLOT) // RIM >= 2
    margin = (lane < RIM) | (lane >= LANES - RIM)

    def put(ref, index, k, both, main):
        ref[index] = jnp.where(margin, lane_roll(both, -(SLOT * k + SLOT // 2)), main[index])

    for t in range(n_trac):
        both = jnp.where(at_west, strips[0].lam[t][0], strips[1].lam[t][0])
        for k in range(lev):
            put(adj_t, (t, k), k, both, main_t)
    for ref, main, *sides in zip((adj_e, adj_n), (main_e, main_n), *(s.gradients() for s in strips)):
        both = jnp.where(at_west, *sides)
        for k in range(lev):
            put(ref, (k,), k, both, main)


def call(body, outs, args, scratch=(), space=pltpu.VMEM):
    shapes = [s if hasattr(s, "dtype") else jax.ShapeDtypeStruct(s, F32) for s in outs]
    return pl.pallas_call(
        body,
        out_shape=shapes,
        in_specs=[pl.BlockSpec(memory_space=space)] * len(args),
        out_specs=[pl.BlockSpec(memory_space=pltpu.VMEM)] * len(outs),
        scratch_shapes=[pltpu.VMEM(s, F32) if isinstance(s, tuple) else s for s in scratch],
        compiler_params=pltpu.CompilerParams(vmem_limit_bytes=VMEM),
    )(*args)


def adjoint(tracers, cotangent, east_vel, north_vel, sea_mask, level_count):
    n_trac, lev, rows, cols = tracers.shape
    assert (rows, cols, lev * SLOT) == (ROWS, LANES, LANES)
    n_lon, n_lat = lax.axis_size("lon"), lax.axis_size("lat")
    assert n_lat % 2 == 0
    n_pairs = (n_trac + 1) * lev + 1
    n_fields = 2 * n_trac + 3
    n_sent = -(-n_fields * RIM // SLOT)
    tile = (rows, cols)

    def swap_a(x):
        return lax.ppermute(x, "lat", [(j, j ^ 1) for j in range(n_lat)])

    def swap_b(x):
        pairs = []
        for i in range(n_lon):
            for j in range(n_lat):
                end = j in (0, n_lat - 1)
                to = (i ^ 1, j) if end else (i, ((j + 1) ^ 1) - 1)
                pairs.append((i * n_lat + j, to[0] * n_lat + to[1]))
        return lax.ppermute(x, ("lon", "lat"), pairs)

    def shift(x, by):
        return lax.ppermute(x, "lon", [(i, (i + by) % n_lon) for i in range(n_lon)])

    args = (tracers, cotangent, east_vel, north_vel, sea_mask, level_count)
    args = [pltpu.with_memory_space_constraint(a, pltpu.HBM) for a in args]
    *args, pair_a, pair_b, to_west, to_east, edge = call(
        pack_kernel,
        [jax.ShapeDtypeStruct(a.shape, a.dtype) for a in args]
        + [(n_pairs,) + tile] * 2
        + [(n_sent,) + tile] * 2
        + [(n_fields,) + tile],
        args,
        [pltpu.SemaphoreType.DMA((len(args),))],
        pltpu.HBM,
    )
    from_west = shift(to_east, 1)
    from_east = shift(to_west, -1)
    pair_b = swap_b(pair_b)
    pair_a = swap_a(pair_a)
    corner_a, corner_b = call(corner_kernel, [(n_sent,) + tile] * 2, (from_west, from_east))
    corner_a = swap_a(corner_a)
    corner_b = swap_b(corner_b)
    outs = [tracers.shape, east_vel.shape, north_vel.shape]
    per_plane = (n_trac, lev) + tile
    near = call(
        near_kernel,
        outs + [(STEPS - 1,) + per_plane] * 2 + [(n_trac + 2,) + tile],
        (*args, pair_a),
        [(4,) + per_plane, (STEPS, 2) + per_plane, (len(COEFS), lev, 2) + tile],
    )
    *main, edge_rim = call(
        far_kernel,
        outs + [(n_fields,) + tile],
        (*args, pair_b, *near),
        [(4,) + per_plane, (STEPS, 2) + per_plane, (len(COEFS), lev) + tile, (2, lev) + tile],
    )
    return tuple(
        call(edge_kernel, outs, (edge, edge_rim, from_west, from_east, corner_a, corner_b, *main))
    )


def solution(mesh):
    state, flat, cell = P(None, None, "lat", "lon"), P(None, "lat", "lon"), P("lat", "lon")
    return jax.shard_map(
        adjoint,
        mesh=mesh,
        in_specs=(state, state, flat, flat, cell, cell),
        out_specs=(state, flat, flat),
        check_vma=False,
    )
```

time: 16.2 us -> 16.1 us (level)
  waiting for transfers between devices: 3.33 us -> 2.53 us
  Pallas kernels: 3.77 us -> 4.49 us
    ppermute x2, waiting for transfers between devices: 1.42 us -> 0.63 us  [swap_b(): return lax.ppermute(x, ('lon', 'lat'), pairs)]
    pallas_call x4 -> x5, Pallas kernels: 3.77 us -> 4.49 us  [call(): pl.pallas_call(body, out_shape=shapes, in_specs=[pl.BlockSpec(memory_spac...]
  transfers between devices with their start and end apart: 6 -> 6, of which waited for: 2 -> 2; matrix products, arithmetic and copies ran while one was open for 0% -> 0% of each run, Pallas kernels for 7% -> 12%
where the time goes in v3:
time: 16.1 us; the launch traced here: 16 us
  starting transfers between devices  8.27 us (51%)
  Pallas kernels  4.49 us (28%)
  waiting for transfers between devices  2.53 us (16%)
  between operations  0.69 us (4%)
    pallas_call x5, Pallas kernels, call(): pl.pallas_call(body, out_shape=shapes, in_specs=[pl.BlockSpec(memory_spac...  4.49 us
    ppermute x2, starting transfers between devices, shift(): return lax.ppermute(x, 'lon', [(i, (i + by) % n_lon) for i in range(n_lon)])  3.82 us
    ppermute x2, starting transfers between devices, swap_b(): return lax.ppermute(x, ('lon', 'lat'), pairs)  3.82 us
    ppermute x2, waiting for transfers between devices, shift(): return lax.ppermute(x, 'lon', [(i, (i + by) % n_lon) for i in range(n_lon)])  1.9 us
    ppermute x2, starting transfers between devices, swap_a(): return lax.ppermute(x, 'lat', [(j, j ^ 1) for j in range(n_lat)])  0.63 us
    ppermute x2, waiting for transfers between devices, swap_b(): return lax.ppermute(x, ('lon', 'lat'), pairs)  0.63 us
  transfers between devices with their start and end apart: 6, of which 2 were waited for; matrix products, arithmetic and copies ran while one was open for 0% of the time, Pallas kernels for 12%

profile of v3, /device:TPU:0, one launch (start us, length us, event | category | flops | bytes accessed | tf_op | source)
XLA Modules:
  0.0 16.0 jit_solution(560288921519169711)
XLA Ops:
  0.6 1.2 %shard_map.85 = (f32[3,8,8,128]{3,2,1,0:T(8,128)S(1)}, f32[3,8,8,128]{3,2,1,0:T(8,128)S(1)}, f32[8,8,128]{2,1,0:T(8,128)S(1)}, f32[8,8,128]{2,1,0:T(8,128)S(1)},...) custom-call(f32[3,8,8,128]{3,2,1,0:T(8,128)} %refs_0_.1, ...), custom_call_target="tpu_custom_call" | custom-call | tf_op jit(solution)/shard_map/pallas_call | solution.py:475
  1.8 0.6 %collective-permute-start.1 = (f32[33,8,128]{2,1,0:T(8,128)S(1)}, f32[33,8,128]{2,1,0:T(8,128)S(1)}, u32[]{:S(2)}, u32[]{:S(2)}) collective-permute-start(f32[33,8,128]{2,1,0:T(8,128)S(1)} %get-tuple-element.34), channel_id=1, source_target_pairs={{0,1},{1,0},{2,3},{3,2},{4,5},{5,4},{6,7},{7,6},{8,9},{9,8},{10,11... | collective-permute-start | bytes 405512 | tf_op jit(solution)/shard_map/ppermute | solution.py:496
  2.4 2.6 %collective-permute-start = (f32[33,8,128]{2,1,0:T(8,128)S(1)}, f32[33,8,128]{2,1,0:T(8,128)S(1)}, u32[]{:S(2)}, u32[]{:S(2)}) collective-permute-start(f32[33,8,128]{2,1,0:T(8,128)S(1)} %get-tuple-element.33), channel_id=1, source_target_pairs={{0,8},{1,2},{2,1},{3,4},{4,3},{5,6},{6,5},{7,15},{8,0},{9,10},{10,... | collective-permute-start | bytes 405512 | tf_op jit(solution)/shard_map/ppermute | solution.py:505
  5.0 0.1 collective-permute-start.2
  5.1 3.8 %collective-permute-start.3 = (f32[3,8,128]{2,1,0:T(8,128)S(1)}, f32[3,8,128]{2,1,0:T(8,128)S(1)}, u32[]{:S(2)}, u32[]{:S(2)}) collective-permute-start(f32[3,8,128]{2,1,0:T(8,128)S(1)} %get-tuple-element.43), channel_id=1, source_target_pairs={{0,24},{8,0},{16,8},{24,16},{1,25},{9,1},{17,9},{25,17},{2,26},{10... | collective-permute-start | bytes 36872 | tf_op jit(solution)/shard_map/ppermute | solution.py:508
  8.9 1.9 %collective-permute-done.2.from_west = f32[3,8,128]{2,1,0:T(8,128)S(1)} collective-permute-done((f32[3,8,128]{2,1,0:T(8,128)S(1)}, f32[3,8,128]{2,1,0:T(8,128)S(1)}, u32[]{:S(2)}, u32[]{:S(2)}) %collective-permute-start.2) | collective-permute-done | bytes 12320 | tf_op jit(solution)/shard_map/ppermute | solution.py:508
  10.8 0.0 collective-permute-done.3.from_east
  10.8 0.1 collective-permute-start.4
  10.9 1.2 %collective-permute-start.5 = (f32[3,8,128]{2,1,0:T(8,128)S(1)}, f32[3,8,128]{2,1,0:T(8,128)S(1)}, u32[]{:S(2)}, u32[]{:S(2)}) collective-permute-start(f32[3,8,128]{2,1,0:T(8,128)S(1)} %get-tuple-element.45), channel_id=1, source_target_pairs={{0,8},{1,2},{2,1},{3,4},{4,3},{5,6},{6,5},{7,15},{8,0},{9,10},{10,... | collective-permute-start | bytes 36872 | tf_op jit(solution)/shard_map/ppermute | solution.py:505
  12.0 0.0 collective-permute-done.1.pair_a
  12.0 1.2 %shard_map.86 = (f32[3,8,8,128]{3,2,1,0:T(8,128)S(1)}, f32[8,8,128]{2,1,0:T(8,128)S(1)}, f32[8,8,128]{2,1,0:T(8,128)S(1)}, f32[3,3,8,8,128]{4,3,2,1,0:T(8,128)S(...) custom-call(f32[3,8,8,128]{3,2,1,0:T(8,128)S(1)} %get-tuple-element.27.trac.refs_0_, ...), custom_call_target="tpu_custom_call" | custom-call | tf_op jit(solution)/shard_map/pallas_call | solution.py:475
  13.2 0.0 collective-permute-done.refs_6_
  13.2 0.8 %shard_map.87 = (f32[3,8,8,128]{3,2,1,0:T(8,128)S(1)}, f32[8,8,128]{2,1,0:T(8,128)S(1)}, f32[8,8,128]{2,1,0:T(8,128)S(1)}, f32[9,8,128]{2,1,0:T(8,128)S(1)}) custom-call(f32[3,8,8,128]{3,2,1,0:T(8,128)S(1)} %get-tuple-element.27.trac.refs_0_, f32[3,8,8,128]{3,2,1,0:T(8,128)S(1)} %get-tuple-element.28.cot.refs_1_, ...), custom_call_target="tpu_custom_call" | custom-call | tf_op jit(solution)/shard_map/pallas_call | solution.py:475
  14.0 0.0 collective-permute-done.4.corner_a
  14.0 0.6 %collective-permute-done.5.corner_b = f32[3,8,128]{2,1,0:T(8,128)S(1)} collective-permute-done((f32[3,8,128]{2,1,0:T(8,128)S(1)}, f32[3,8,128]{2,1,0:T(8,128)S(1)}, u32[]{:S(2)}, u32[]{:S(2)}) %collective-permute-start.5) | collective-permute-done | bytes 12320 | tf_op jit(solution)/shard_map/ppermute | solution.py:505
  14.6 1.4 %shard_map.89 = (f32[3,8,8,128]{3,2,1,0:T(8,128)}, f32[8,8,128]{2,1,0:T(8,128)}, f32[8,8,128]{2,1,0:T(8,128)}) custom-call(f32[9,8,128]{2,1,0:T(8,128)S(1)} %get-tuple-element.26.edge, f32[9,8,128]{2,1,0:T(8,128)S(1)} %get-tuple-element.41.edge_rim, f32[3,8,128]{2,1,0:T(8,128)S(1)} %collective-permute-done.2.from_west, ...), custom_call_target="tpu_custom_call" | custom-call | tf_op jit(solution)/shard_map/pallas_call | solution.py:475
  (1 shorter events, 0.0 us)
Async XLA Ops:
  1.8 10.2 %collective-permute-start.1 = (f32[33,8,128]{2,1,0:T(8,128)S(1)}, f32[33,8,128]{2,1,0:T(8,128)S(1)}, u32[]{:S(2)}, u32[]{:S(2)}) collective-permute-start(f32[33,8,128]{2,1,0:T(8,128)S(1)} %get-tuple-element.34), channel_id=1, source_target_pairs={{0,1},{1,0},{2,3},{3,2},{4,5},{5,4},{6,7},{7,6},{8,9},{9,8},{10,11... | collective-permute-start | bytes 405512 | tf_op jit(solution)/shard_map/ppermute | solution.py:496
  2.4 10.8 %collective-permute-start = (f32[33,8,128]{2,1,0:T(8,128)S(1)}, f32[33,8,128]{2,1,0:T(8,128)S(1)}, u32[]{:S(2)}, u32[]{:S(2)}) collective-permute-start(f32[33,8,128]{2,1,0:T(8,128)S(1)} %get-tuple-element.33), channel_id=1, source_target_pairs={{0,8},{1,2},{2,1},{3,4},{4,3},{5,6},{6,5},{7,15},{8,0},{9,10},{10,... | collective-permute-start | bytes 405512 | tf_op jit(solution)/shard_map/ppermute | solution.py:505
  5.0 5.7 %collective-permute-start.2 = (f32[3,8,128]{2,1,0:T(8,128)S(1)}, f32[3,8,128]{2,1,0:T(8,128)S(1)}, u32[]{:S(2)}, u32[]{:S(2)}) collective-permute-start(f32[3,8,128]{2,1,0:T(8,128)S(1)} %get-tuple-element.42), channel_id=1, source_target_pairs={{0,8},{8,16},{16,24},{24,0},{1,9},{9,17},{17,25},{25,1},{2,10},{10... | collective-permute-start | bytes 36872 | tf_op jit(solution)/shard_map/ppermute | solution.py:508
  5.1 5.7 %collective-permute-start.3 = (f32[3,8,128]{2,1,0:T(8,128)S(1)}, f32[3,8,128]{2,1,0:T(8,128)S(1)}, u32[]{:S(2)}, u32[]{:S(2)}) collective-permute-start(f32[3,8,128]{2,1,0:T(8,128)S(1)} %get-tuple-element.43), channel_id=1, source_target_pairs={{0,24},{8,0},{16,8},{24,16},{1,25},{9,1},{17,9},{25,17},{2,26},{10... | collective-permute-start | bytes 36872 | tf_op jit(solution)/shard_map/ppermute | solution.py:508
  10.8 3.2 %collective-permute-start.4 = (f32[3,8,128]{2,1,0:T(8,128)S(1)}, f32[3,8,128]{2,1,0:T(8,128)S(1)}, u32[]{:S(2)}, u32[]{:S(2)}) collective-permute-start(f32[3,8,128]{2,1,0:T(8,128)S(1)} %get-tuple-element.44), channel_id=1, source_target_pairs={{0,1},{1,0},{2,3},{3,2},{4,5},{5,4},{6,7},{7,6},{8,9},{9,8},{10,11... | collective-permute-start | bytes 36872 | tf_op jit(solution)/shard_map/ppermute | solution.py:496
  10.9 3.8 %collective-permute-start.5 = (f32[3,8,128]{2,1,0:T(8,128)S(1)}, f32[3,8,128]{2,1,0:T(8,128)S(1)}, u32[]{:S(2)}, u32[]{:S(2)}) collective-permute-start(f32[3,8,128]{2,1,0:T(8,128)S(1)} %get-tuple-element.45), channel_id=1, source_target_pairs={{0,8},{1,2},{2,1},{3,4},{4,3},{5,6},{6,5},{7,15},{8,0},{9,10},{10,... | collective-permute-start | bytes 36872 | tf_op jit(solution)/shard_map/ppermute | solution.py:505

commit v4 on v3

--- a/solution.py
+++ b/solution.py
@@ -272,8 +272,18 @@
             adj_n[k] = acc_n
 
 
+def march(steps):
+    for i in range(steps):
+        yield lambda part: part.backward(i)
+        yield lambda part: part.forward(i)
+        for step in range(steps):
+            if max(step, steps - 1 - step) == i:
+                yield lambda part: part.collect(step)
+
+
 class Far:
-    def __init__(self, args, pair_b, past, past_adj, state, sums, coef, acc):
+    def __init__(self, args, pair_b, past, past_adj, state, sums, slopes, coef, acc):
+        self.slopes, self.started = slopes, False
         self.trac, self.cot, east_vel, north_vel, mask, count = args
         self.past, self.past_adj, self.state, self.sums, self.coef, self.acc = past, past_adj, state, sums, coef, acc
         n_trac, lev = self.n_trac, self.lev = self.trac.shape[:2]
@@ -336,17 +346,22 @@
         src, dst = 2 + done % 2, 2 + (done + 1) % 2
         own = self.past_adj.at[done - 1] if done else self.cot
         for k in range(self.lev):
-            acc_e = acc_n = None
             for t in range(self.n_trac):
                 x, beyond = self.state[src, t, k], own[t, k]
                 e, n = east(x), self.north(x, beyond)
                 about = x, e, west(x), n, self.south(x, beyond)
                 self.state[dst, t, k] = self.apply(src, t, k, about, BACKWARD)
-                acc_e = add(acc_e, self.sums[step, 0, t, k] * (e - x))
-                acc_n = add(acc_n, self.sums[step, 1, t, k] * (n - x))
-            if done:
-                acc_e, acc_n = acc_e + self.acc[0, k], acc_n + self.acc[1, k]
-            self.acc[0, k], self.acc[1, k] = acc_e, acc_n
+                self.slopes[step, 0, t, k] = e - x
+                self.slopes[step, 1, t, k] = n - x
+
+    def collect(self, step):
+        for k in range(self.lev):
+            for i in range(2):
+                total = self.acc[i, k] if self.started else None
+                for t in range(self.n_trac):
+                    total = add(total, self.sums[step, i, t, k] * self.slopes[step, i, t, k])
+                self.acc[i, k] = total
+        self.started = True
 
     def merged(self, t, k, near):
         return jnp.where(self.rim, row_roll(self.state[2 + STEPS % 2, t, k], RIM), near)
@@ -380,7 +395,7 @@
         self.made = coefficients(wet, up, down, field(2 * n_trac), field(2 * n_trac + 1))
         self.state = [field(t) for t in range(n_trac)]
         self.lam = [field(n_trac + t) for t in range(n_trac)]
-        self.sums, self.acc_e, self.acc_n = [], None, None
+        self.sums, self.slopes, self.acc_e, self.acc_n = [], {}, None, None
 
     def near(self, x):
         n, s = north(*x, self.last), south(*x, self.first)
@@ -402,11 +417,13 @@
     def backward(self, done):
         step = STEPS - 1 - done
         about = [self.near(x) for x in self.lam]
-        for (sum_e, sum_n), a in zip(self.sums[step], about):
-            x, e, n = a[0][0], a[1][0], a[3][0]
-            self.acc_e = add(self.acc_e, sum_e * (e - x))
-            self.acc_n = add(self.acc_n, sum_n * (n - x))
+        self.slopes[step] = [(a[1][0] - a[0][0], a[3][0] - a[0][0]) for a in about]
         self.lam = [self.apply(a, BACKWARD, (0, 1) if step else (0,)) for a in about]
+
+    def collect(self, step):
+        for (sum_e, sum_n), (slope_e, slope_n) in zip(self.sums[step], self.slopes[step]):
+            self.acc_e = add(self.acc_e, sum_e * slope_e)
+            self.acc_n = add(self.acc_n, sum_n * slope_n)
 
     def gradients(self):
         own = self.made[0]
@@ -416,7 +433,7 @@
 def far_kernel(*refs):
     args, refs = refs[:6], refs[6:]
     pair_b, near_t, near_e, near_n, past, past_adj, edge_a = refs[:7]
-    adj_t, adj_e, adj_n, edge_rim, state, sums, coef, acc = refs[7:]
+    adj_t, adj_e, adj_n, edge_rim, state, sums, slopes, coef, acc = refs[7:]
     n_trac, lev = near_t.shape[:2]
 
     for i, b in enumerate(packed_edges(pair_b, n_trac, lev)):
@@ -427,11 +444,9 @@
             edge_rim[2 * n_trac], edge_rim[2 * n_trac + 1] = p, q
         else:
             edge_rim[2 * n_trac + 2] = p
-    far = Far(args, pair_b, past, past_adj, state, sums, coef, acc)
-    for step in range(STEPS):
-        far.forward(step)
-    for done in range(STEPS):
-        far.backward(done)
+    far = Far(args, pair_b, past, past_adj, state, sums, slopes, coef, acc)
+    for part in march(STEPS):
+        part(far)
     for k in range(lev):
         for t in range(n_trac):
             adj_t[t, k] = far.merged(t, k, near_t[t, k])
@@ -446,12 +461,9 @@
         Strip(side, n_trac, lev, edge, edge_rim, sent, [c[side] for c in corners])
         for side, sent in enumerate((from_west, from_east))
     ]
-    for step in range(STEPS):
-        for part in strips:
-            part.forward(step)
-    for done in range(STEPS):
-        for part in strips:
-            part.backward(done)
+    for part in march(STEPS):
+        for strip in strips:
+            part(strip)
 
     lane = iota(1)
     at_west = (lane % SLOT) // RIM >= 2
@@ -522,9 +534,9 @@
     from_west = shift(to_east, 1)
     from_east = shift(to_west, -1)
     pair_b = swap_b(pair_b)
-    pair_a = swap_a(pair_a)
     corner_a, corner_b = call(corner_kernel, [(n_sent,) + tile] * 2, (from_west, from_east))
-    corner_a = swap_a(corner_a)
+    both_a = swap_a(jnp.concatenate([pair_a, corner_a]))
+    pair_a, corner_a = both_a, both_a[n_pairs:]
     corner_b = swap_b(corner_b)
     outs = [tracers.shape, east_vel.shape, north_vel.shape]
     per_plane = (n_trac, lev) + tile
@@ -538,7 +550,7 @@
         far_kernel,
         outs + [(n_fields,) + tile],
         (*args, pair_b, *near),
-        [(4,) + per_plane, (STEPS, 2) + per_plane, (len(COEFS), lev) + tile, (2, lev) + tile],
+        [(4,) + per_plane] + [(STEPS, 2) + per_plane] * 2 + [(len(COEFS), lev) + tile, (2, lev) + tile],
     )
     return tuple(
         call(edge_kernel, outs, (edge, edge_rim, from_west, from_east, corner_a, corner_b, *main))

time: 16.1 us -> 16.9 us (1.050)
  the two profiles are of different devices: /device:TPU:0 before, /device:TPU:27 now
where the time goes in v4:
time: 16.9 us; the launch traced here: 16.8 us
  starting transfers between devices  6.2 us (37%)
  waiting for transfers between devices  5.49 us (32%)
  Pallas kernels  4.39 us (26%)
  between operations  0.68 us (4%)
    pallas_call x5, Pallas kernels, call(): pl.pallas_call(body, out_shape=shapes, in_specs=[pl.BlockSpec(memory_spac...  4.39 us
    ppermute x2, waiting for transfers between devices, shift(): return lax.ppermute(x, 'lon', [(i, (i + by) % n_lon) for i in range(n_lon)])  2.94 us
    ppermute x2, starting transfers between devices, swap_b(): return lax.ppermute(x, ('lon', 'lat'), pairs)  2.64 us
    ppermute x2, waiting for transfers between devices, swap_b(): return lax.ppermute(x, ('lon', 'lat'), pairs)  2.55 us
    ppermute x1, starting transfers between devices, swap_a(): return lax.ppermute(x, 'lat', [(j, j ^ 1) for j in range(n_lat)])  2.05 us
    ppermute x2, starting transfers between devices, shift(): return lax.ppermute(x, 'lon', [(i, (i + by) % n_lon) for i in range(n_lon)])  1.51 us
  transfers between devices with their start and end apart: 5, of which 3 were waited for; matrix products, arithmetic and copies ran while one was open for 0% of the time, Pallas kernels for 11%

profile of v4, /device:TPU:27, one launch (start us, length us, event | category | flops | bytes accessed | tf_op | source)
XLA Modules:
  0.0 16.8 jit_solution(2987651052543458760)
XLA Ops:
  0.6 1.2 %shard_map.85 = (f32[3,8,8,128]{3,2,1,0:T(8,128)S(1)}, f32[3,8,8,128]{3,2,1,0:T(8,128)S(1)}, f32[8,8,128]{2,1,0:T(8,128)S(1)}, f32[8,8,128]{2,1,0:T(8,128)S(1)},...) custom-call(f32[3,8,8,128]{3,2,1,0:T(8,128)} %refs_0_.1, ...), custom_call_target="tpu_custom_call" | custom-call | tf_op jit(solution)/shard_map/pallas_call | solution.py:487
  1.8 0.1 collective-permute-start.1
  1.9 1.5 %collective-permute-start.2 = (f32[3,8,128]{2,1,0:T(8,128)S(1)}, f32[3,8,128]{2,1,0:T(8,128)S(1)}, u32[]{:S(2)}, u32[]{:S(2)}) collective-permute-start(f32[3,8,128]{2,1,0:T(8,128)S(1)} %get-tuple-element.36), channel_id=1, source_target_pairs={{0,24},{8,0},{16,8},{24,16},{1,25},{9,1},{17,9},{25,17},{2,26},{10... | collective-permute-start | bytes 36872 | tf_op jit(solution)/shard_map/ppermute | solution.py:520
  3.4 1.1 %collective-permute-done.1.from_west = f32[3,8,128]{2,1,0:T(8,128)S(1)} collective-permute-done((f32[3,8,128]{2,1,0:T(8,128)S(1)}, f32[3,8,128]{2,1,0:T(8,128)S(1)}, u32[]{:S(2)}, u32[]{:S(2)}) %collective-permute-start.1) | collective-permute-done | bytes 12320 | tf_op jit(solution)/shard_map/ppermute | solution.py:520
  4.4 1.9 %collective-permute-done.2.from_east = f32[3,8,128]{2,1,0:T(8,128)S(1)} collective-permute-done((f32[3,8,128]{2,1,0:T(8,128)S(1)}, f32[3,8,128]{2,1,0:T(8,128)S(1)}, u32[]{:S(2)}, u32[]{:S(2)}) %collective-permute-start.2) | collective-permute-done | bytes 12320 | tf_op jit(solution)/shard_map/ppermute | solution.py:520
  6.3 2.0 %collective-permute-start.3 = (f32[36,8,128]{2,1,0:T(8,128)S(1)}, f32[36,8,128]{2,1,0:T(8,128)S(1)}, u32[]{:S(2)}, u32[]{:S(2)}) collective-permute-start(f32[36,8,128]{2,1,0:T(8,128)S(1)} %pad_maximum_fusion), channel_id=1, source_target_pairs={{0,1},{1,0},{2,3},{3,2},{4,5},{5,4},{6,7},{7,6},{8,9},{9,8},{10,11... | collective-permute-start | bytes 442376 | tf_op jit(solution)/shard_map/ppermute | solution.py:508
  8.4 1.2 %collective-permute-start = (f32[33,8,128]{2,1,0:T(8,128)S(1)}, f32[33,8,128]{2,1,0:T(8,128)S(1)}, u32[]{:S(2)}, u32[]{:S(2)}) collective-permute-start(f32[33,8,128]{2,1,0:T(8,128)S(1)} %get-tuple-element.33), channel_id=1, source_target_pairs={{0,8},{1,2},{2,1},{3,4},{4,3},{5,6},{6,5},{7,15},{8,0},{9,10},{10,... | collective-permute-start | bytes 405512 | tf_op jit(solution)/shard_map/ppermute | solution.py:517
  9.6 1.5 %collective-permute-start.4 = (f32[3,8,128]{2,1,0:T(8,128)S(1)}, f32[3,8,128]{2,1,0:T(8,128)S(1)}, u32[]{:S(2)}, u32[]{:S(2)}) collective-permute-start(f32[3,8,128]{2,1,0:T(8,128)S(1)} %get-tuple-element.45), channel_id=1, source_target_pairs={{0,8},{1,2},{2,1},{3,4},{4,3},{5,6},{6,5},{7,15},{8,0},{9,10},{10,... | collective-permute-start | bytes 36872 | tf_op jit(solution)/shard_map/ppermute | solution.py:517
  11.0 0.0 collective-permute-done.3.pair_a
  11.0 1.2 %shard_map.87 = (f32[3,8,8,128]{3,2,1,0:T(8,128)S(1)}, f32[8,8,128]{2,1,0:T(8,128)S(1)}, f32[8,8,128]{2,1,0:T(8,128)S(1)}, f32[3,3,8,8,128]{4,3,2,1,0:T(8,128)S(...) custom-call(f32[3,8,8,128]{3,2,1,0:T(8,128)S(1)} %get-tuple-element.27.trac.refs_0_, ...), custom_call_target="tpu_custom_call" | custom-call | tf_op jit(solution)/shard_map/pallas_call | solution.py:487
  12.2 2.5 %collective-permute-done.refs_6_ = f32[33,8,128]{2,1,0:T(8,128)S(1)} collective-permute-done((f32[33,8,128]{2,1,0:T(8,128)S(1)}, f32[33,8,128]{2,1,0:T(8,128)S(1)}, u32[]{:S(2)}, u32[]{:S(2)}) %collective-permute-start) | collective-permute-done | bytes 135200 | tf_op jit(solution)/shard_map/ppermute | solution.py:517
  14.7 0.7 %shard_map.88 = (f32[3,8,8,128]{3,2,1,0:T(8,128)S(1)}, f32[8,8,128]{2,1,0:T(8,128)S(1)}, f32[8,8,128]{2,1,0:T(8,128)S(1)}, f32[9,8,128]{2,1,0:T(8,128)S(1)}) custom-call(f32[3,8,8,128]{3,2,1,0:T(8,128)S(1)} %get-tuple-element.27.trac.refs_0_, f32[3,8,8,128]{3,2,1,0:T(8,128)S(1)} %get-tuple-element.28.cot.refs_1_, ...), custom_call_target="tpu_custom_call" | custom-call | tf_op jit(solution)/shard_map/pallas_call | solution.py:487
  15.5 0.0 collective-permute-done.4.corner_b
  15.5 1.3 %shard_map.89 = (f32[3,8,8,128]{3,2,1,0:T(8,128)}, f32[8,8,128]{2,1,0:T(8,128)}, f32[8,8,128]{2,1,0:T(8,128)}) custom-call(f32[9,8,128]{2,1,0:T(8,128)S(1)} %get-tuple-element.26.edge, f32[9,8,128]{2,1,0:T(8,128)S(1)} %get-tuple-element.44.edge_rim, f32[3,8,128]{2,1,0:T(8,128)S(1)} %collective-permute-done.1.from_west, ...), custom_call_target="tpu_custom_call" | custom-call | tf_op jit(solution)/shard_map/pallas_call | solution.py:487
  (3 shorter events, 0.0 us)
Async XLA Ops:
  1.8 2.6 %collective-permute-start.1 = (f32[3,8,128]{2,1,0:T(8,128)S(1)}, f32[3,8,128]{2,1,0:T(8,128)S(1)}, u32[]{:S(2)}, u32[]{:S(2)}) collective-permute-start(f32[3,8,128]{2,1,0:T(8,128)S(1)} %get-tuple-element.35), channel_id=1, source_target_pairs={{0,8},{8,16},{16,24},{24,0},{1,9},{9,17},{17,25},{25,1},{2,10},{10... | collective-permute-start | bytes 36872 | tf_op jit(solution)/shard_map/ppermute | solution.py:520
  1.9 4.4 %collective-permute-start.2 = (f32[3,8,128]{2,1,0:T(8,128)S(1)}, f32[3,8,128]{2,1,0:T(8,128)S(1)}, u32[]{:S(2)}, u32[]{:S(2)}) collective-permute-start(f32[3,8,128]{2,1,0:T(8,128)S(1)} %get-tuple-element.36), channel_id=1, source_target_pairs={{0,24},{8,0},{16,8},{24,16},{1,25},{9,1},{17,9},{25,17},{2,26},{10... | collective-permute-start | bytes 36872 | tf_op jit(solution)/shard_map/ppermute | solution.py:520
  6.3 4.7 %collective-permute-start.3 = (f32[36,8,128]{2,1,0:T(8,128)S(1)}, f32[36,8,128]{2,1,0:T(8,128)S(1)}, u32[]{:S(2)}, u32[]{:S(2)}) collective-permute-start(f32[36,8,128]{2,1,0:T(8,128)S(1)} %pad_maximum_fusion), channel_id=1, source_target_pairs={{0,1},{1,0},{2,3},{3,2},{4,5},{5,4},{6,7},{7,6},{8,9},{9,8},{10,11... | collective-permute-start | bytes 442376 | tf_op jit(solution)/shard_map/ppermute | solution.py:508
  8.4 6.4 %collective-permute-start = (f32[33,8,128]{2,1,0:T(8,128)S(1)}, f32[33,8,128]{2,1,0:T(8,128)S(1)}, u32[]{:S(2)}, u32[]{:S(2)}) collective-permute-start(f32[33,8,128]{2,1,0:T(8,128)S(1)} %get-tuple-element.33), channel_id=1, source_target_pairs={{0,8},{1,2},{2,1},{3,4},{4,3},{5,6},{6,5},{7,15},{8,0},{9,10},{10,... | collective-permute-start | bytes 405512 | tf_op jit(solution)/shard_map/ppermute | solution.py:517
  9.6 5.9 %collective-permute-start.4 = (f32[3,8,128]{2,1,0:T(8,128)S(1)}, f32[3,8,128]{2,1,0:T(8,128)S(1)}, u32[]{:S(2)}, u32[]{:S(2)}) collective-permute-start(f32[3,8,128]{2,1,0:T(8,128)S(1)} %get-tuple-element.45), channel_id=1, source_target_pairs={{0,8},{1,2},{2,1},{3,4},{4,3},{5,6},{6,5},{7,15},{8,0},{9,10},{10,... | collective-permute-start | bytes 36872 | tf_op jit(solution)/shard_map/ppermute | solution.py:517

commit v5 on v4

--- a/solution.py
+++ b/solution.py
@@ -75,7 +75,9 @@
 
 def pack_kernel(*refs):
     args, here, (pair_a, pair_b, to_west, to_east, edge, sems) = refs[:6], refs[6:12], refs[12:]
-    copies = [pltpu.make_async_copy(a, b, sems.at[i]) for i, (a, b) in enumerate(zip(args, here))]
+    parts = [(a.at[t], b.at[t]) for a, b in zip(args[:2], here[:2]) for t in range(a.shape[0])]
+    parts += list(zip(args[2:], here[2:]))
+    copies = [pltpu.make_async_copy(a, b, sems.at[i]) for i, (a, b) in enumerate(parts)]
     for copy in copies:
         copy.start()
     for copy in copies:
@@ -281,11 +283,23 @@
                 yield lambda part: part.collect(step)
 
 
+def beyond_kernel(trac, cot, past, past_adj, beyond, beside):
+    first = iota(0) == 0
+    n_trac, lev = trac.shape[:2]
+    for i, (start, later) in enumerate(((trac, past), (cot, past_adj))):
+        for t in range(n_trac):
+            for k in range(lev):
+                beside[i, t, k] = row_roll(start[t, k], RIM)
+                for step in range(STEPS):
+                    x = later[step - 1, t, k] if step else start[t, k]
+                    beyond[i, step, t, k] = jnp.where(first, row_roll(x, -3), row_roll(x, 3))
+
+
 class Far:
-    def __init__(self, args, pair_b, past, past_adj, state, sums, slopes, coef, acc):
+    def __init__(self, args, pair_b, beyond, beside, state, sums, slopes, coef, acc):
         self.slopes, self.started = slopes, False
         self.trac, self.cot, east_vel, north_vel, mask, count = args
-        self.past, self.past_adj, self.state, self.sums, self.coef, self.acc = past, past_adj, state, sums, coef, acc
+        self.beyond, self.state, self.sums, self.coef, self.acc = beyond, state, sums, coef, acc
         n_trac, lev = self.n_trac, self.lev = self.trac.shape[:2]
         sub = iota(0)
         self.first, self.last = sub == 0, sub == ROWS - 1
@@ -293,11 +307,11 @@
 
         def both(index, p, q):
             x = pair_b[index]
-            return self.join(row_roll(x, RIM), p), self.join(x, q)
+            return jnp.where(self.rim, row_roll(x, RIM), p), jnp.where(self.rim, x, q)
 
         for t in range(n_trac):
             for k in range(lev):
-                state[0, t, k], state[2, t, k] = both(t * lev + k, self.trac[t, k], self.cot[t, k])
+                state[0, t, k], state[2, t, k] = both(t * lev + k, beside[0, t, k], beside[1, t, k])
         place = lax.axis_index("lat")
         outside = (place == 0) | (place == lax.axis_size("lat") - 1)
         count_own = wet_count(mask[...], count[...])
@@ -306,7 +320,7 @@
         own = [jnp.where(count_own > k, 1.0, 0.0) for k in range(lev)]
         far = [jnp.where(count_far > k, 1.0, 0.0) for k in range(lev)]
         for k in range(lev):
-            u, v = both(n_trac * lev + k, east_vel[k], north_vel[k])
+            u, v = both(n_trac * lev + k, row_roll(east_vel[k], RIM), row_roll(north_vel[k], RIM))
             beyond = velocity_terms(own[k], own[k], row_roll(own[k], -1), north_vel[k], north_vel[k])
             made = velocity_terms(far[k], east(far[k]), self.north(far[k], own[k]), u, v)
             rs, ss = (self.south(made[x], beyond[x]) for x in "rs")
@@ -323,6 +337,12 @@
     def south(self, x, beyond):
         return jnp.where(self.first, row_roll(beyond, -3), row_roll(x, 1))
 
+    def next_row(self, x, beyond):
+        return jnp.where(self.last, beyond, row_roll(x, -1))
+
+    def row_before(self, x, beyond):
+        return jnp.where(self.first, beyond, row_roll(x, 1))
+
     def apply(self, buf, t, k, about, names):
         up = self.state[buf, t, k + 1] if k + 1 < self.lev else None
         down = self.state[buf, t, k - 1] if k else None
@@ -330,26 +350,24 @@
 
     def forward(self, step):
         src, dst = step % 2, (step + 1) % 2
-        own = self.past.at[step - 1] if step else self.trac
         for k in range(self.lev):
             for t in range(self.n_trac):
-                x, beyond = self.state[src, t, k], own[t, k]
-                e, n = east(x), self.north(x, beyond)
+                x, beyond = self.state[src, t, k], self.beyond[0, step, t, k]
+                e, n = east(x), self.next_row(x, beyond)
                 self.sums[step, 0, t, k] = x + e
                 self.sums[step, 1, t, k] = x + n
                 if step < STEPS - 1:
-                    about = x, e, west(x), n, self.south(x, beyond)
+                    about = x, e, west(x), n, self.row_before(x, beyond)
                     self.state[dst, t, k] = self.apply(src, t, k, about, FORWARD)
 
     def backward(self, done):
         step = STEPS - 1 - done
         src, dst = 2 + done % 2, 2 + (done + 1) % 2
-        own = self.past_adj.at[done - 1] if done else self.cot
         for k in range(self.lev):
             for t in range(self.n_trac):
-                x, beyond = self.state[src, t, k], own[t, k]
-                e, n = east(x), self.north(x, beyond)
-                about = x, e, west(x), n, self.south(x, beyond)
+                x, beyond = self.state[src, t, k], self.beyond[1, done, t, k]
+                e, n = east(x), self.next_row(x, beyond)
+                about = x, e, west(x), n, self.row_before(x, beyond)
                 self.state[dst, t, k] = self.apply(src, t, k, about, BACKWARD)
                 self.slopes[step, 0, t, k] = e - x
                 self.slopes[step, 1, t, k] = n - x
@@ -432,7 +450,7 @@
 
 def far_kernel(*refs):
     args, refs = refs[:6], refs[6:]
-    pair_b, near_t, near_e, near_n, past, past_adj, edge_a = refs[:7]
+    pair_b, near_t, near_e, near_n, edge_a, beyond, beside = refs[:7]
     adj_t, adj_e, adj_n, edge_rim, state, sums, slopes, coef, acc = refs[7:]
     n_trac, lev = near_t.shape[:2]
 
@@ -444,7 +462,7 @@
             edge_rim[2 * n_trac], edge_rim[2 * n_trac + 1] = p, q
         else:
             edge_rim[2 * n_trac + 2] = p
-    far = Far(args, pair_b, past, past_adj, state, sums, slopes, coef, acc)
+    far = Far(args, pair_b, beyond, beside, state, sums, slopes, coef, acc)
     for part in march(STEPS):
         part(far)
     for k in range(lev):
@@ -528,7 +546,7 @@
         + [(n_sent,) + tile] * 2
         + [(n_fields,) + tile],
         args,
-        [pltpu.SemaphoreType.DMA((len(args),))],
+        [pltpu.SemaphoreType.DMA((2 * n_trac + 4,))],
         pltpu.HBM,
     )
     from_west = shift(to_east, 1)
@@ -546,10 +564,14 @@
         (*args, pair_a),
         [(4,) + per_plane, (STEPS, 2) + per_plane, (len(COEFS), lev, 2) + tile],
     )
+    near_t, near_e, near_n, past, past_adj, edge_a = near
+    turned = call(
+        beyond_kernel, [(2, STEPS) + per_plane, (2,) + per_plane], (args[0], args[1], past, past_adj)
+    )
     *main, edge_rim = call(
         far_kernel,
         outs + [(n_fields,) + tile],
-        (*args, pair_b, *near),
+        (*args, pair_b, near_t, near_e, near_n, edge_a, *turned),
         [(4,) + per_plane] + [(STEPS, 2) + per_plane] * 2 + [(len(COEFS), lev) + tile, (2, lev) + tile],
     )
     return tuple(

time: 16.9 us -> 16.9 us (level)
    pallas_call x5 -> x6, Pallas kernels: 4.39 us -> 4.42 us  [call(): pl.pallas_call(body, out_shape=shapes, in_specs=[pl.BlockSpec(memory_spac...]
  transfers between devices with their start and end apart: 5 -> 5, of which waited for: 3 -> 3; matrix products, arithmetic and copies ran while one was open for 0% -> 0% of each run, Pallas kernels for 11% -> 12%
where the time goes in v5:
time: 16.9 us; the launch traced here: 16.7 us
  starting transfers between devices  6.2 us (37%)
  waiting for transfers between devices  5.39 us (32%)
  Pallas kernels  4.42 us (26%)
  between operations  0.7 us (4%)
    pallas_call x6, Pallas kernels, call(): pl.pallas_call(body, out_shape=shapes, in_specs=[pl.BlockSpec(memory_spac...  4.42 us
    ppermute x2, waiting for transfers between devices, shift(): return lax.ppermute(x, 'lon', [(i, (i + by) % n_lon) for i in range(n_lon)])  2.94 us
    ppermute x2, starting transfers between devices, swap_b(): return lax.ppermute(x, ('lon', 'lat'), pairs)  2.64 us
    ppermute x2, waiting for transfers between devices, swap_b(): return lax.ppermute(x, ('lon', 'lat'), pairs)  2.45 us
    ppermute x1, starting transfers between devices, swap_a(): return lax.ppermute(x, 'lat', [(j, j ^ 1) for j in range(n_lat)])  2.05 us
    ppermute x2, starting transfers between devices, shift(): return lax.ppermute(x, 'lon', [(i, (i + by) % n_lon) for i in range(n_lon)])  1.51 us
  transfers between devices with their start and end apart: 5, of which 3 were waited for; matrix products, arithmetic and copies ran while one was open for 0% of the time, Pallas kernels for 12%

profile of v5, /device:TPU:27, one launch (start us, length us, event | category | flops | bytes accessed | tf_op | source)
XLA Modules:
  0.0 16.7 jit_solution(3135214005294629544)
XLA Ops:
  0.6 1.2 %shard_map.85 = (f32[3,8,8,128]{3,2,1,0:T(8,128)S(1)}, f32[3,8,8,128]{3,2,1,0:T(8,128)S(1)}, f32[8,8,128]{2,1,0:T(8,128)S(1)}, f32[8,8,128]{2,1,0:T(8,128)S(1)},...) custom-call(f32[3,8,8,128]{3,2,1,0:T(8,128)} %refs_0_.1, ...), custom_call_target="tpu_custom_call" | custom-call | tf_op jit(solution)/shard_map/pallas_call | solution.py:505
  1.8 0.1 collective-permute-start.1
  1.9 1.5 %collective-permute-start.2 = (f32[3,8,128]{2,1,0:T(8,128)S(1)}, f32[3,8,128]{2,1,0:T(8,128)S(1)}, u32[]{:S(2)}, u32[]{:S(2)}) collective-permute-start(f32[3,8,128]{2,1,0:T(8,128)S(1)} %get-tuple-element.38), channel_id=1, source_target_pairs={{0,24},{8,0},{16,8},{24,16},{1,25},{9,1},{17,9},{25,17},{2,26},{10... | collective-permute-start | bytes 36872 | tf_op jit(solution)/shard_map/ppermute | solution.py:538
  3.3 1.1 %collective-permute-done.1.from_west = f32[3,8,128]{2,1,0:T(8,128)S(1)} collective-permute-done((f32[3,8,128]{2,1,0:T(8,128)S(1)}, f32[3,8,128]{2,1,0:T(8,128)S(1)}, u32[]{:S(2)}, u32[]{:S(2)}) %collective-permute-start.1) | collective-permute-done | bytes 12320 | tf_op jit(solution)/shard_map/ppermute | solution.py:538
  4.4 1.9 %collective-permute-done.2.from_east = f32[3,8,128]{2,1,0:T(8,128)S(1)} collective-permute-done((f32[3,8,128]{2,1,0:T(8,128)S(1)}, f32[3,8,128]{2,1,0:T(8,128)S(1)}, u32[]{:S(2)}, u32[]{:S(2)}) %collective-permute-start.2) | collective-permute-done | bytes 12320 | tf_op jit(solution)/shard_map/ppermute | solution.py:538
  6.3 2.0 %collective-permute-start.3 = (f32[36,8,128]{2,1,0:T(8,128)S(1)}, f32[36,8,128]{2,1,0:T(8,128)S(1)}, u32[]{:S(2)}, u32[]{:S(2)}) collective-permute-start(f32[36,8,128]{2,1,0:T(8,128)S(1)} %pad_maximum_fusion), channel_id=1, source_target_pairs={{0,1},{1,0},{2,3},{3,2},{4,5},{5,4},{6,7},{7,6},{8,9},{9,8},{10,11... | collective-permute-start | bytes 442376 | tf_op jit(solution)/shard_map/ppermute | solution.py:526
  8.3 1.2 %collective-permute-start = (f32[33,8,128]{2,1,0:T(8,128)S(1)}, f32[33,8,128]{2,1,0:T(8,128)S(1)}, u32[]{:S(2)}, u32[]{:S(2)}) collective-permute-start(f32[33,8,128]{2,1,0:T(8,128)S(1)} %get-tuple-element.35), channel_id=1, source_target_pairs={{0,8},{1,2},{2,1},{3,4},{4,3},{5,6},{6,5},{7,15},{8,0},{9,10},{10,... | collective-permute-start | bytes 405512 | tf_op jit(solution)/shard_map/ppermute | solution.py:535
  9.5 1.5 %collective-permute-start.4 = (f32[3,8,128]{2,1,0:T(8,128)S(1)}, f32[3,8,128]{2,1,0:T(8,128)S(1)}, u32[]{:S(2)}, u32[]{:S(2)}) collective-permute-start(f32[3,8,128]{2,1,0:T(8,128)S(1)} %get-tuple-element.49), channel_id=1, source_target_pairs={{0,8},{1,2},{2,1},{3,4},{4,3},{5,6},{6,5},{7,15},{8,0},{9,10},{10,... | collective-permute-start | bytes 36872 | tf_op jit(solution)/shard_map/ppermute | solution.py:535
  11.0 0.0 collective-permute-done.3.pair_a
  11.0 1.2 %shard_map.87 = (f32[3,8,8,128]{3,2,1,0:T(8,128)S(1)}, f32[8,8,128]{2,1,0:T(8,128)S(1)}, f32[8,8,128]{2,1,0:T(8,128)S(1)}, f32[3,3,8,8,128]{4,3,2,1,0:T(8,128)S(...) custom-call(f32[3,8,8,128]{3,2,1,0:T(8,128)S(1)} %get-tuple-element.29.trac.refs_0_, ...), custom_call_target="tpu_custom_call" | custom-call | tf_op jit(solution)/shard_map/pallas_call | solution.py:505
  12.1 0.1 shard_map.88
  12.3 2.4 %collective-permute-done.refs_6_ = f32[33,8,128]{2,1,0:T(8,128)S(1)} collective-permute-done((f32[33,8,128]{2,1,0:T(8,128)S(1)}, f32[33,8,128]{2,1,0:T(8,128)S(1)}, u32[]{:S(2)}, u32[]{:S(2)}) %collective-permute-start) | collective-permute-done | bytes 135200 | tf_op jit(solution)/shard_map/ppermute | solution.py:535
  14.7 0.7 %shard_map.89 = (f32[3,8,8,128]{3,2,1,0:T(8,128)S(1)}, f32[8,8,128]{2,1,0:T(8,128)S(1)}, f32[8,8,128]{2,1,0:T(8,128)S(1)}, f32[9,8,128]{2,1,0:T(8,128)S(1)}) custom-call(f32[3,8,8,128]{3,2,1,0:T(8,128)S(1)} %get-tuple-element.29.trac.refs_0_, f32[3,8,8,128]{3,2,1,0:T(8,128)S(1)} %get-tuple-element.30.cot.refs_1_, ...), custom_call_target="tpu_custom_call" | custom-call | tf_op jit(solution)/shard_map/pallas_call | solution.py:505
  15.4 0.0 collective-permute-done.4.corner_b
  15.4 1.3 %shard_map.90 = (f32[3,8,8,128]{3,2,1,0:T(8,128)}, f32[8,8,128]{2,1,0:T(8,128)}, f32[8,8,128]{2,1,0:T(8,128)}) custom-call(f32[9,8,128]{2,1,0:T(8,128)S(1)} %get-tuple-element.28.edge, f32[9,8,128]{2,1,0:T(8,128)S(1)} %get-tuple-element.48.edge_rim, f32[3,8,128]{2,1,0:T(8,128)S(1)} %collective-permute-done.1.from_west, ...), custom_call_target="tpu_custom_call" | custom-call | tf_op jit(solution)/shard_map/pallas_call | solution.py:505
  (3 shorter events, 0.0 us)
Async XLA Ops:
  1.8 2.6 %collective-permute-start.1 = (f32[3,8,128]{2,1,0:T(8,128)S(1)}, f32[3,8,128]{2,1,0:T(8,128)S(1)}, u32[]{:S(2)}, u32[]{:S(2)}) collective-permute-start(f32[3,8,128]{2,1,0:T(8,128)S(1)} %get-tuple-element.37), channel_id=1, source_target_pairs={{0,8},{8,16},{16,24},{24,0},{1,9},{9,17},{17,25},{25,1},{2,10},{10... | collective-permute-start | bytes 36872 | tf_op jit(solution)/shard_map/ppermute | solution.py:538
  1.9 4.4 %collective-permute-start.2 = (f32[3,8,128]{2,1,0:T(8,128)S(1)}, f32[3,8,128]{2,1,0:T(8,128)S(1)}, u32[]{:S(2)}, u32[]{:S(2)}) collective-permute-start(f32[3,8,128]{2,1,0:T(8,128)S(1)} %get-tuple-element.38), channel_id=1, source_target_pairs={{0,24},{8,0},{16,8},{24,16},{1,25},{9,1},{17,9},{25,17},{2,26},{10... | collective-permute-start | bytes 36872 | tf_op jit(solution)/shard_map/ppermute | solution.py:538
  6.3 4.7 %collective-permute-start.3 = (f32[36,8,128]{2,1,0:T(8,128)S(1)}, f32[36,8,128]{2,1,0:T(8,128)S(1)}, u32[]{:S(2)}, u32[]{:S(2)}) collective-permute-start(f32[36,8,128]{2,1,0:T(8,128)S(1)} %pad_maximum_fusion), channel_id=1, source_target_pairs={{0,1},{1,0},{2,3},{3,2},{4,5},{5,4},{6,7},{7,6},{8,9},{9,8},{10,11... | collective-permute-start | bytes 442376 | tf_op jit(solution)/shard_map/ppermute | solution.py:526
  8.3 6.4 %collective-permute-start = (f32[33,8,128]{2,1,0:T(8,128)S(1)}, f32[33,8,128]{2,1,0:T(8,128)S(1)}, u32[]{:S(2)}, u32[]{:S(2)}) collective-permute-start(f32[33,8,128]{2,1,0:T(8,128)S(1)} %get-tuple-element.35), channel_id=1, source_target_pairs={{0,8},{1,2},{2,1},{3,4},{4,3},{5,6},{6,5},{7,15},{8,0},{9,10},{10,... | collective-permute-start | bytes 405512 | tf_op jit(solution)/shard_map/ppermute | solution.py:535
  9.5 5.9 %collective-permute-start.4 = (f32[3,8,128]{2,1,0:T(8,128)S(1)}, f32[3,8,128]{2,1,0:T(8,128)S(1)}, u32[]{:S(2)}, u32[]{:S(2)}) collective-permute-start(f32[3,8,128]{2,1,0:T(8,128)S(1)} %get-tuple-element.49), channel_id=1, source_target_pairs={{0,8},{1,2},{2,1},{3,4},{4,3},{5,6},{6,5},{7,15},{8,0},{9,10},{10,... | collective-permute-start | bytes 36872 | tf_op jit(solution)/shard_map/ppermute | solution.py:535

commit v6 on v5

--- a/solution.py
+++ b/solution.py
@@ -283,9 +283,16 @@
                 yield lambda part: part.collect(step)
 
 
-def beyond_kernel(trac, cot, past, past_adj, beyond, beside):
+def beyond_kernel(trac, cot, past, past_adj, edge, from_west, from_east, beyond, beside, strip_own):
     first = iota(0) == 0
     n_trac, lev = trac.shape[:2]
+    n_fields = edge.shape[0]
+    for side, sent in enumerate((from_west, from_east)):
+        from_side = (iota(1) % SLOT) // RIM == 1 + side
+        for f in range(n_fields):
+            d, g = divmod(f, SLOT // RIM)
+            shift = 0 if f == n_fields - 1 and g == 0 else 8 - RIM * g
+            strip_own[side, f] = jnp.where(from_side, lane_roll(sent[d], shift), edge[f])
     for i, (start, later) in enumerate(((trac, past), (cot, past_adj))):
         for t in range(n_trac):
             for k in range(lev):
@@ -390,9 +397,9 @@
 
 
 class Strip:
-    def __init__(self, side, n_trac, lev, edge, rims, sent, corners):
+    def __init__(self, side, n_trac, lev, strip_own, rims, corners):
         self.n_trac = n_trac
-        n_fields = edge.shape[0]
+        n_fields = strip_own.shape[1]
         sub, lane = iota(0), iota(1)
         self.first, self.last = sub == 0, sub == ROWS - 1
         level = lane // SLOT
@@ -401,7 +408,7 @@
         def field(f):
             d, g = divmod(f, SLOT // RIM)
             shift = 0 if f == n_fields - 1 and g == 0 else 8 - RIM * g
-            own = jnp.where(from_side, lane_roll(sent[d], shift), edge[f])
+            own = strip_own[side, f]
             rim = jnp.where(from_side, lane_roll(corners[d], shift), rims[f])
             return own, rim
 
@@ -472,13 +479,10 @@
         adj_n[k] = far.merged_gradient(1, k, near_n[k])
 
 
-def edge_kernel(edge, edge_rim, from_west, from_east, corner_a, corner_b, main_t, main_e, main_n, adj_t, adj_e, adj_n):
+def edge_kernel(strip_own, edge_rim, corner_a, corner_b, main_t, main_e, main_n, adj_t, adj_e, adj_n):
     n_trac, lev = main_t.shape[:2]
-    corners = [unpair(corner_a[d], corner_b[d]) for d in range(from_west.shape[0])]
-    strips = [
-        Strip(side, n_trac, lev, edge, edge_rim, sent, [c[side] for c in corners])
-        for side, sent in enumerate((from_west, from_east))
-    ]
+    corners = [unpair(corner_a[d], corner_b[d]) for d in range(corner_a.shape[0])]
+    strips = [Strip(side, n_trac, lev, strip_own, edge_rim, [c[side] for c in corners]) for side in range(2)]
     for part in march(STEPS):
         for strip in strips:
             part(strip)
@@ -565,8 +569,10 @@
         [(4,) + per_plane, (STEPS, 2) + per_plane, (len(COEFS), lev, 2) + tile],
     )
     near_t, near_e, near_n, past, past_adj, edge_a = near
-    turned = call(
-        beyond_kernel, [(2, STEPS) + per_plane, (2,) + per_plane], (args[0], args[1], past, past_adj)
+    *turned, strip_own = call(
+        beyond_kernel,
+        [(2, STEPS) + per_plane, (2,) + per_plane, (2, n_fields) + tile],
+        (args[0], args[1], past, past_adj, edge, from_west, from_east),
     )
     *main, edge_rim = call(
         far_kernel,
@@ -575,7 +581,7 @@
         [(4,) + per_plane] + [(STEPS, 2) + per_plane] * 2 + [(len(COEFS), lev) + tile, (2, lev) + tile],
     )
     return tuple(
-        call(edge_kernel, outs, (edge, edge_rim, from_west, from_east, corner_a, corner_b, *main))
+        call(edge_kernel, outs, (strip_own, edge_rim, corner_a, corner_b, *main))
     )
 
 

time: 16.9 us -> 16.9 us (level)
  no operation moved by 1% of the time
where the time goes in v6:
time: 16.9 us; the launch traced here: 16.7 us
  starting transfers between devices  6.2 us (37%)
  waiting for transfers between devices  5.39 us (32%)
  Pallas kernels  4.45 us (26%)
  between operations  0.69 us (4%)
    pallas_call x6, Pallas kernels, call(): pl.pallas_call(body, out_shape=shapes, in_specs=[pl.BlockSpec(memory_spac...  4.45 us
    ppermute x2, waiting for transfers between devices, shift(): return lax.ppermute(x, 'lon', [(i, (i + by) % n_lon) for i in range(n_lon)])  2.94 us
    ppermute x2, starting transfers between devices, swap_b(): return lax.ppermute(x, ('lon', 'lat'), pairs)  2.64 us
    ppermute x2, waiting for transfers between devices, swap_b(): return lax.ppermute(x, ('lon', 'lat'), pairs)  2.44 us
    ppermute x1, starting transfers between devices, swap_a(): return lax.ppermute(x, 'lat', [(j, j ^ 1) for j in range(n_lat)])  2.05 us
    ppermute x2, starting transfers between devices, shift(): return lax.ppermute(x, 'lon', [(i, (i + by) % n_lon) for i in range(n_lon)])  1.51 us
  transfers between devices with their start and end apart: 5, of which 3 were waited for; matrix products, arithmetic and copies ran while one was open for 0% of the time, Pallas kernels for 12%

profile of v6, /device:TPU:27, one launch (start us, length us, event | category | flops | bytes accessed | tf_op | source)
XLA Modules:
  0.0 16.7 jit_solution(7882415345013174495)
XLA Ops:
  0.6 1.2 %shard_map.85 = (f32[3,8,8,128]{3,2,1,0:T(8,128)S(1)}, f32[3,8,8,128]{3,2,1,0:T(8,128)S(1)}, f32[8,8,128]{2,1,0:T(8,128)S(1)}, f32[8,8,128]{2,1,0:T(8,128)S(1)},...) custom-call(f32[3,8,8,128]{3,2,1,0:T(8,128)} %refs_0_.1, ...), custom_call_target="tpu_custom_call" | custom-call | tf_op jit(solution)/shard_map/pallas_call | solution.py:509
  1.8 0.1 collective-permute-start
  1.9 1.5 %collective-permute-start.1 = (f32[3,8,128]{2,1,0:T(8,128)S(1)}, f32[3,8,128]{2,1,0:T(8,128)S(1)}, u32[]{:S(2)}, u32[]{:S(2)}) collective-permute-start(f32[3,8,128]{2,1,0:T(8,128)S(1)} %get-tuple-element.37), channel_id=1, source_target_pairs={{0,24},{8,0},{16,8},{24,16},{1,25},{9,1},{17,9},{25,17},{2,26},{10... | collective-permute-start | bytes 36872 | tf_op jit(solution)/shard_map/ppermute | solution.py:542
  3.3 1.1 %collective-permute-done.from_west = f32[3,8,128]{2,1,0:T(8,128)S(1)} collective-permute-done((f32[3,8,128]{2,1,0:T(8,128)S(1)}, f32[3,8,128]{2,1,0:T(8,128)S(1)}, u32[]{:S(2)}, u32[]{:S(2)}) %collective-permute-start) | collective-permute-done | bytes 12320 | tf_op jit(solution)/shard_map/ppermute | solution.py:542
  4.4 1.9 %collective-permute-done.1.from_east = f32[3,8,128]{2,1,0:T(8,128)S(1)} collective-permute-done((f32[3,8,128]{2,1,0:T(8,128)S(1)}, f32[3,8,128]{2,1,0:T(8,128)S(1)}, u32[]{:S(2)}, u32[]{:S(2)}) %collective-permute-start.1) | collective-permute-done | bytes 12320 | tf_op jit(solution)/shard_map/ppermute | solution.py:542
  6.3 2.0 %collective-permute-start.2 = (f32[36,8,128]{2,1,0:T(8,128)S(1)}, f32[36,8,128]{2,1,0:T(8,128)S(1)}, u32[]{:S(2)}, u32[]{:S(2)}) collective-permute-start(f32[36,8,128]{2,1,0:T(8,128)S(1)} %pad_maximum_fusion), channel_id=1, source_target_pairs={{0,1},{1,0},{2,3},{3,2},{4,5},{5,4},{6,7},{7,6},{8,9},{9,8},{10,11... | collective-permute-start | bytes 442376 | tf_op jit(solution)/shard_map/ppermute | solution.py:530
  8.3 1.2 %collective-permute-start.3 = (f32[33,8,128]{2,1,0:T(8,128)S(1)}, f32[33,8,128]{2,1,0:T(8,128)S(1)}, u32[]{:S(2)}, u32[]{:S(2)}) collective-permute-start(f32[33,8,128]{2,1,0:T(8,128)S(1)} %get-tuple-element.43), channel_id=1, source_target_pairs={{0,8},{1,2},{2,1},{3,4},{4,3},{5,6},{6,5},{7,15},{8,0},{9,10},{10,... | collective-permute-start | bytes 405512 | tf_op jit(solution)/shard_map/ppermute | solution.py:539
  9.5 1.5 %collective-permute-start.4 = (f32[3,8,128]{2,1,0:T(8,128)S(1)}, f32[3,8,128]{2,1,0:T(8,128)S(1)}, u32[]{:S(2)}, u32[]{:S(2)}) collective-permute-start(f32[3,8,128]{2,1,0:T(8,128)S(1)} %get-tuple-element.51), channel_id=1, source_target_pairs={{0,8},{1,2},{2,1},{3,4},{4,3},{5,6},{6,5},{7,15},{8,0},{9,10},{10,... | collective-permute-start | bytes 36872 | tf_op jit(solution)/shard_map/ppermute | solution.py:539
  11.0 0.0 collective-permute-done.2.pair_a
  11.0 1.2 %shard_map.87 = (f32[3,8,8,128]{3,2,1,0:T(8,128)S(1)}, f32[8,8,128]{2,1,0:T(8,128)S(1)}, f32[8,8,128]{2,1,0:T(8,128)S(1)}, f32[3,3,8,8,128]{4,3,2,1,0:T(8,128)S(...) custom-call(f32[3,8,8,128]{3,2,1,0:T(8,128)S(1)} %get-tuple-element.29.trac.refs_0_, ...), custom_call_target="tpu_custom_call" | custom-call | tf_op jit(solution)/shard_map/pallas_call | solution.py:509
  12.2 0.1 shard_map.88
  12.3 2.4 %collective-permute-done.3.refs_6_ = f32[33,8,128]{2,1,0:T(8,128)S(1)} collective-permute-done((f32[33,8,128]{2,1,0:T(8,128)S(1)}, f32[33,8,128]{2,1,0:T(8,128)S(1)}, u32[]{:S(2)}, u32[]{:S(2)}) %collective-permute-start.3) | collective-permute-done | bytes 135200 | tf_op jit(solution)/shard_map/ppermute | solution.py:539
  14.7 0.7 %shard_map.89 = (f32[3,8,8,128]{3,2,1,0:T(8,128)S(1)}, f32[8,8,128]{2,1,0:T(8,128)S(1)}, f32[8,8,128]{2,1,0:T(8,128)S(1)}, f32[9,8,128]{2,1,0:T(8,128)S(1)}) custom-call(f32[3,8,8,128]{3,2,1,0:T(8,128)S(1)} %get-tuple-element.29.trac.refs_0_, f32[3,8,8,128]{3,2,1,0:T(8,128)S(1)} %get-tuple-element.30.cot.refs_1_, ...), custom_call_target="tpu_custom_call" | custom-call | tf_op jit(solution)/shard_map/pallas_call | solution.py:509
  15.4 0.0 collective-permute-done.4.corner_b
  15.4 1.3 %shard_map.90 = (f32[3,8,8,128]{3,2,1,0:T(8,128)}, f32[8,8,128]{2,1,0:T(8,128)}, f32[8,8,128]{2,1,0:T(8,128)}) custom-call(f32[2,9,8,128]{3,2,1,0:T(8,128)S(1)} %get-tuple-element.42.strip_own, f32[9,8,128]{2,1,0:T(8,128)S(1)} %get-tuple-element.50.edge_rim, f32[3,8,128]{2,1,0:T(8,128)S(1)} %slice.4.corner_a, ...), custom_call_target="tpu_custom_call" | custom-call | tf_op jit(solution)/shard_map/pallas_call | solution.py:509
  (3 shorter events, 0.0 us)
Async XLA Ops:
  1.8 2.6 %collective-permute-start = (f32[3,8,128]{2,1,0:T(8,128)S(1)}, f32[3,8,128]{2,1,0:T(8,128)S(1)}, u32[]{:S(2)}, u32[]{:S(2)}) collective-permute-start(f32[3,8,128]{2,1,0:T(8,128)S(1)} %get-tuple-element.36), channel_id=1, source_target_pairs={{0,8},{8,16},{16,24},{24,0},{1,9},{9,17},{17,25},{25,1},{2,10},{10... | collective-permute-start | bytes 36872 | tf_op jit(solution)/shard_map/ppermute | solution.py:542
  1.9 4.4 %collective-permute-start.1 = (f32[3,8,128]{2,1,0:T(8,128)S(1)}, f32[3,8,128]{2,1,0:T(8,128)S(1)}, u32[]{:S(2)}, u32[]{:S(2)}) collective-permute-start(f32[3,8,128]{2,1,0:T(8,128)S(1)} %get-tuple-element.37), channel_id=1, source_target_pairs={{0,24},{8,0},{16,8},{24,16},{1,25},{9,1},{17,9},{25,17},{2,26},{10... | collective-permute-start | bytes 36872 | tf_op jit(solution)/shard_map/ppermute | solution.py:542
  6.3 4.7 %collective-permute-start.2 = (f32[36,8,128]{2,1,0:T(8,128)S(1)}, f32[36,8,128]{2,1,0:T(8,128)S(1)}, u32[]{:S(2)}, u32[]{:S(2)}) collective-permute-start(f32[36,8,128]{2,1,0:T(8,128)S(1)} %pad_maximum_fusion), channel_id=1, source_target_pairs={{0,1},{1,0},{2,3},{3,2},{4,5},{5,4},{6,7},{7,6},{8,9},{9,8},{10,11... | collective-permute-start | bytes 442376 | tf_op jit(solution)/shard_map/ppermute | solution.py:530
  8.3 6.4 %collective-permute-start.3 = (f32[33,8,128]{2,1,0:T(8,128)S(1)}, f32[33,8,128]{2,1,0:T(8,128)S(1)}, u32[]{:S(2)}, u32[]{:S(2)}) collective-permute-start(f32[33,8,128]{2,1,0:T(8,128)S(1)} %get-tuple-element.43), channel_id=1, source_target_pairs={{0,8},{1,2},{2,1},{3,4},{4,3},{5,6},{6,5},{7,15},{8,0},{9,10},{10,... | collective-permute-start | bytes 405512 | tf_op jit(solution)/shard_map/ppermute | solution.py:539
  9.5 5.9 %collective-permute-start.4 = (f32[3,8,128]{2,1,0:T(8,128)S(1)}, f32[3,8,128]{2,1,0:T(8,128)S(1)}, u32[]{:S(2)}, u32[]{:S(2)}) collective-permute-start(f32[3,8,128]{2,1,0:T(8,128)S(1)} %get-tuple-element.51), channel_id=1, source_target_pairs={{0,8},{1,2},{2,1},{3,4},{4,3},{5,6},{6,5},{7,15},{8,0},{9,10},{10,... | collective-permute-start | bytes 36872 | tf_op jit(solution)/shard_map/ppermute | solution.py:539
